TPU v7x, 128 devices: a whole 4x4x4 slice. The times are simulated.
128 devices in a mesh: row: 8 (over x, core), col: 16 (over z, y).
Axes of the slice: x: 4, y: 4, z: 4, core: 2. Of those that a mesh axis runs over, the one named last changes fastest.
Arguments:
- currents: bfloat16 [49152, 256], P(('row', 'col')), may hold values from -6 to 6
- incidence: int32 [2, 49152], P(None, ('row', 'col')), may hold values from 0 to 32767, as said below
- centroids: int32 [3, 32768], P(None, ('row', 'col')), may hold values from 0 to 255, as said below
- sweep_weights: float32 [2], replicated, may hold values from 0.2 to 0.6
Outputs:
- updated: bfloat16 [49152, 256], P(('row', 'col'))
- potentials: bfloat16 [32768, 256], P(('row', 'col'))
Inputs may be any that keep to these rules, and one draw needn't show every extreme that they name: `incidence`: triangles o * 256 to (o + 1) * 256 - 1 form owner block o. Counting both rows, the edges of one device name at most 16 triangles of any one owner block, and exactly 16 of some block on every device. `centroids`: first two rows from 0 to 255, third row from 0 to 3.
All inputs are finite; a program needn't handle non-finite values.
Results may differ from a plain program's by a relative error of at most 0.006.
Values may be sent and summed in bfloat16 or wider, within the bound.
A program may use at most 128 MiB of HBM per device.

v0:
```python
import math

import jax
import jax.numpy as jnp
from jax import lax
from jax.sharding import PartitionSpec as P

WAVE = 0.19634954084936207
SOFT = 1.0
SPACING = 0.2


def tile_pair(row_pts, col_pts):
    dx = (row_pts[0][:, None] - col_pts[0][None, :]).astype(jnp.float32)
    dy = (row_pts[1][:, None] - col_pts[1][None, :]).astype(jnp.float32)
    dz = (row_pts[2][:, None] - col_pts[2][None, :]).astype(jnp.float32)
    radius = jnp.sqrt(dx * dx + dy * dy + dz * dz + SOFT * SOFT)
    scaled = SPACING / radius
    return (
        (scaled * jnp.cos(WAVE * radius)).astype(jnp.bfloat16),
        (-scaled * jnp.sin(WAVE * radius)).astype(jnp.bfloat16),
    )


def blend(real_part, imag_part):
    half = real_part.shape[1] // 2
    return jnp.concatenate(
        [real_part[:, :half] - imag_part[:, half:], real_part[:, half:] + imag_part[:, :half]], 1
    )


def row_block(row_count, col_count):
    target = max(1, 2**20 // max(1, col_count))
    power = 1 << target.bit_length() - 1
    return max(min(512, row_count), math.gcd(row_count, power))


def per_device(currents, incidence, centroids, sweep_weights):
    n_row = lax.axis_size("row")
    n_col = lax.axis_size("col")
    devices = n_row * n_col
    tri_dev = centroids.shape[1]
    edge_dev = currents.shape[0]
    width = currents.shape[1]
    slots = 8 * tri_dev // devices
    cells = devices * slots
    row_points = lax.all_gather(centroids, "col", axis=1, tiled=True)
    col_points = lax.all_gather(centroids, "row", axis=1, tiled=True)
    row_count = row_points.shape[1]
    triangle = incidence.reshape(-1)
    owner = triangle // tri_dev
    local = triangle % tri_dev
    owner_hits = (owner[:, None] == jnp.arange(devices, dtype=jnp.int32)[None, :]).astype(jnp.int32)
    position = jnp.cumsum(owner_hits, axis=0)
    rank = jnp.sum(owner_hits * position, axis=1) - 1
    slot = owner * slots + rank
    labels = jnp.zeros((cells,), jnp.int32).at[slot].set(local + 1)
    current = currents
    potential = None
    for sweep in range(sweep_weights.shape[0]):
        signed = jnp.concatenate([current, -current], 0)
        outgoing = jnp.zeros((cells, width), jnp.bfloat16).at[slot].set(signed)
        route_flat_vals = outgoing.reshape(devices, slots, width)
        flat_marks = labels.reshape(devices, slots)
        got_vals = lax.all_to_all(
            route_flat_vals, ("row", "col"), split_axis=0, concat_axis=0, tiled=True
        )
        got_marks = lax.all_to_all(
            flat_marks, ("row", "col"), split_axis=0, concat_axis=0, tiled=True
        )
        arrived = got_vals.reshape(cells, width)
        arrived_marks = got_marks.reshape(cells)
        slot_map = (
            arrived_marks[:, None] == jnp.arange(1, tri_dev + 1, dtype=jnp.int32)[None, :]
        ).astype(jnp.bfloat16)
        charges = lax.dot_general(
            slot_map, arrived, (((0,), (0,)), ((), ())), preferred_element_type=jnp.float32
        ).astype(jnp.bfloat16)
        empty = jnp.zeros((row_count, width), jnp.float32)
        piece = lax.all_gather(charges, "row", axis=0, tiled=True)
        block = row_block(row_count, piece.shape[0])
        n_blocks = row_count // block

        def one_block(index):
            points = lax.dynamic_slice_in_dim(row_points, index * block, block, 1)
            g_real, g_imag = tile_pair(points, col_points)
            return blend(
                jnp.dot(g_real, piece, preferred_element_type=jnp.float32),
                jnp.dot(g_imag, piece, preferred_element_type=jnp.float32),
            )

        blocks = lax.map(one_block, jnp.arange(n_blocks, dtype=jnp.int32))
        partial_value = blocks.reshape(empty.shape)
        owned = lax.psum_scatter(partial_value, "col", scatter_dimension=0, tiled=True)
        potential = owned.astype(jnp.bfloat16)
        answers = jnp.dot(slot_map, potential, preferred_element_type=jnp.float32).astype(
            jnp.bfloat16
        )
        flat_vals = answers.reshape(devices, slots, width)
        got = lax.all_to_all(flat_vals, ("row", "col"), split_axis=0, concat_axis=0, tiled=True)
        returned = got.reshape(cells, width)
        picked = returned[slot]
        slope = picked[:edge_dev].astype(jnp.float32) - picked[edge_dev:].astype(jnp.float32)
        current = (current.astype(jnp.float32) - sweep_weights[sweep] * slope).astype(jnp.bfloat16)
    return (current, potential)


def solution(mesh):
    in_specs = (P(("row", "col"), None), P(None, ("row", "col")), P(None, ("row", "col")), P())
    out_specs = (P(("row", "col"), None), P(("row", "col"), None))
    return jax.shard_map(
        per_device, mesh=mesh, in_specs=in_specs, out_specs=out_specs, check_vma=False
    )
```

profile of v0, /device:TPU:0, one launch (start us, length us, event | category | flops | bytes accessed | tf_op | source)
XLA Modules:
  0.0 998.7 jit_solution(10442651588185125750)
XLA Ops:
  77.5 21.7 %all_gather.12 = s32[3,4096]{1,0:T(4,128)S(1)} all-gather(s32[3,256]{1,0:T(4,128)S(1)} %copy-done.2), channel_id=1, replica_groups=mesh['row'=8,'col'=16] {'col'}, dimensions={1}, use_global_device_ids=true | all-gather | bytes 52224 | tf_op jit(solution)/shard_map/all_gather | solution.py:47
  101.5 310.8 %while.20 = (s32[]{:T(128)}, f32[8,512,256]{2,1,0:T(8,128)}, s32[8]{0:T(128)S(1)}, s32[3,4096]{1,0:T(4,128)S(1)}, s32[3,2048]{1,0:T(4,128)S(1)}, /*index=5*/bf16...) while((s32[]{:T(128)}, f32[8,512,256]{2,1,0:T(8,128)}, ...), condition=%wide.region_6.7_spmd, body=%wide.region_5.6_spmd.sunk | while | flops 1108606976 | bytes 7987923 | solution.py:92
  103.2 17.9 %fusion.94 = f32[512,256]{0,1:T(8,128)S(1)} fusion(bf16[2048,256]{1,0:T(8,128)(2,1)S(1)} %get-tuple-element.249, s32[2048]{0:T(1024)S(1)} %bitcast.101, s32[512]{0:T(512)S(1)} %bitcast.115, s32[2048]{0:T(1024)S(1)} %bitcast.103, s32[512]{0:T(512)S(1)} %bitcast.113, s32[2048]{0:T(1024)S(1)} %bitcast.99, s32[512]{0:T(512)S(1)} %bitcast.111), kind=kOutput, calls=%fused_computation.9.clone.1 | convolution fusion | flops 553648128 | bytes 1603584 | tf_op jit(solution)/shard_map/while/body/eval_jaxpr/dot_general | solution.py:88
  159.0 17.8 %fusion.93 = f32[512,256]{0,1:T(8,128)S(1)} fusion(bf16[2048,256]{1,0:T(8,128)(2,1)S(1)} %get-tuple-element.249, s32[2048]{0:T(1024)S(1)} %bitcast.102, s32[512]{0:T(512)S(1)} %bitcast.116, s32[2048]{0:T(1024)S(1)} %bitcast.104, s32[512]{0:T(512)S(1)} %bitcast.114, s32[2048]{0:T(1024)S(1)} %bitcast.100, s32[512]{0:T(512)S(1)} %bitcast.112), kind=kOutput, calls=%fused_computation.10.clone.1 | convolution fusion | flops 554696704 | bytes 1603584 | tf_op jit(solution)/shard_map/while/body/eval_jaxpr/dot_general | solution.py:89
  179.6 17.7 %fusion.94 = f32[512,256]{0,1:T(8,128)S(1)} fusion(bf16[2048,256]{1,0:T(8,128)(2,1)S(1)} %get-tuple-element.249, s32[2048]{0:T(1024)S(1)} %bitcast.101, s32[512]{0:T(512)S(1)} %bitcast.115, s32[2048]{0:T(1024)S(1)} %bitcast.103, s32[512]{0:T(512)S(1)} %bitcast.113, s32[2048]{0:T(1024)S(1)} %bitcast.99, s32[512]{0:T(512)S(1)} %bitcast.111), kind=kOutput, calls=%fused_computation.9.clone.1 | convolution fusion | flops 553648128 | bytes 1603584 | tf_op jit(solution)/shard_map/while/body/eval_jaxpr/dot_general | solution.py:88
  235.3 17.8 %fusion.93 = f32[512,256]{0,1:T(8,128)S(1)} fusion(bf16[2048,256]{1,0:T(8,128)(2,1)S(1)} %get-tuple-element.249, s32[2048]{0:T(1024)S(1)} %bitcast.102, s32[512]{0:T(512)S(1)} %bitcast.116, s32[2048]{0:T(1024)S(1)} %bitcast.104, s32[512]{0:T(512)S(1)} %bitcast.114, s32[2048]{0:T(1024)S(1)} %bitcast.100, s32[512]{0:T(512)S(1)} %bitcast.112), kind=kOutput, calls=%fused_computation.10.clone.1 | convolution fusion | flops 554696704 | bytes 1603584 | tf_op jit(solution)/shard_map/while/body/eval_jaxpr/dot_general | solution.py:89
  255.8 17.7 %fusion.94 = f32[512,256]{0,1:T(8,128)S(1)} fusion(bf16[2048,256]{1,0:T(8,128)(2,1)S(1)} %get-tuple-element.249, s32[2048]{0:T(1024)S(1)} %bitcast.101, s32[512]{0:T(512)S(1)} %bitcast.115, s32[2048]{0:T(1024)S(1)} %bitcast.103, s32[512]{0:T(512)S(1)} %bitcast.113, s32[2048]{0:T(1024)S(1)} %bitcast.99, s32[512]{0:T(512)S(1)} %bitcast.111), kind=kOutput, calls=%fused_computation.9.clone.1 | convolution fusion | flops 553648128 | bytes 1603584 | tf_op jit(solution)/shard_map/while/body/eval_jaxpr/dot_general | solution.py:88
  311.5 17.8 %fusion.93 = f32[512,256]{0,1:T(8,128)S(1)} fusion(bf16[2048,256]{1,0:T(8,128)(2,1)S(1)} %get-tuple-element.249, s32[2048]{0:T(1024)S(1)} %bitcast.102, s32[512]{0:T(512)S(1)} %bitcast.116, s32[2048]{0:T(1024)S(1)} %bitcast.104, s32[512]{0:T(512)S(1)} %bitcast.114, s32[2048]{0:T(1024)S(1)} %bitcast.100, s32[512]{0:T(512)S(1)} %bitcast.112), kind=kOutput, calls=%fused_computation.10.clone.1 | convolution fusion | flops 554696704 | bytes 1603584 | tf_op jit(solution)/shard_map/while/body/eval_jaxpr/dot_general | solution.py:89
  332.0 17.7 %fusion.94 = f32[512,256]{0,1:T(8,128)S(1)} fusion(bf16[2048,256]{1,0:T(8,128)(2,1)S(1)} %get-tuple-element.249, s32[2048]{0:T(1024)S(1)} %bitcast.101, s32[512]{0:T(512)S(1)} %bitcast.115, s32[2048]{0:T(1024)S(1)} %bitcast.103, s32[512]{0:T(512)S(1)} %bitcast.113, s32[2048]{0:T(1024)S(1)} %bitcast.99, s32[512]{0:T(512)S(1)} %bitcast.111), kind=kOutput, calls=%fused_computation.9.clone.1 | convolution fusion | flops 553648128 | bytes 1603584 | tf_op jit(solution)/shard_map/while/body/eval_jaxpr/dot_general | solution.py:88
  387.7 17.8 %fusion.93 = f32[512,256]{0,1:T(8,128)S(1)} fusion(bf16[2048,256]{1,0:T(8,128)(2,1)S(1)} %get-tuple-element.249, s32[2048]{0:T(1024)S(1)} %bitcast.102, s32[512]{0:T(512)S(1)} %bitcast.116, s32[2048]{0:T(1024)S(1)} %bitcast.104, s32[512]{0:T(512)S(1)} %bitcast.114, s32[2048]{0:T(1024)S(1)} %bitcast.100, s32[512]{0:T(512)S(1)} %bitcast.112), kind=kOutput, calls=%fused_computation.10.clone.1 | convolution fusion | flops 554696704 | bytes 1603584 | tf_op jit(solution)/shard_map/while/body/eval_jaxpr/dot_general | solution.py:89
  412.4 75.9 %reduce-scatter.3.cloned.1.call-done = f32[256,256]{1,0:T(8,128)} async-done(((f32[4096,256]{1,0:T(8,128)}), f32[256,256]{1,0:T(8,128)}) %reduce-scatter.3.cloned.1.call-update) | async-done | bytes 262160 | tf_op jit(solution)/shard_map/reduce_scatter | solution.py:94
  499.3 18.3 %all-to-all-done.2 = bf16[128,16,256]{2,1,0:T(8,128)(2,1)S(1)} async-done(((bf16[128,16,256]{2,1,0:T(8,128)(2,1)}), bf16[128,16,256]{2,1,0:T(8,128)(2,1)S(1)}, u32[]{:S(2)}, u32[]{:S(2)}) %all-to-all-start.2) | async-done | bytes 1048608 | tf_op jit(solution)/shard_map/all_to_all | solution.py:100
  527.6 23.0 %all_to_all.30 = bf16[128,16,256]{2,1,0:T(8,128)(2,1)S(1)} all-to-all(bf16[128,16,256]{2,1,0:T(8,128)(2,1)S(1)} %bitcast.95), channel_id=1, replica_groups=mesh['row'=8,'col'=16] {'row','col'}, dimensions={0} | all-to-all | bytes 2097152 | tf_op jit(solution)/shard_map/all_to_all | solution.py:65
  552.4 18.7 %all-gather.5.cloned.1.call-done = bf16[2048,256]{1,0:T(8,128)(2,1)} async-done(((bf16[256,256]{1,0:T(8,128)(2,1)}), bf16[2048,256]{1,0:T(8,128)(2,1)}) %all-gather.5.cloned.1.call-update) | async-done | bytes 1048592 | tf_op jit(solution)/shard_map/all_gather | solution.py:80
  573.4 307.3 %while.21 = (s32[]{:T(128)}, f32[8,512,256]{2,1,0:T(8,128)}, s32[8]{0:T(128)S(1)}, s32[3,4096]{1,0:T(4,128)S(1)}, s32[3,2048]{1,0:T(4,128)S(1)}, /*index=5*/bf16...) while((s32[]{:T(128)}, f32[8,512,256]{2,1,0:T(8,128)}, ...), condition=%wide.region_10.11_spmd, body=%wide.region_9.10_spmd.sunk | while | flops 1108606976 | bytes 7987923 | solution.py:92
  592.6 17.8 %fusion.98 = f32[512,256]{0,1:T(8,128)S(1)} fusion(bf16[2048,256]{1,0:T(8,128)(2,1)S(1)} %get-tuple-element.285, s32[2048]{0:T(1024)S(1)} %bitcast.108, s32[512]{0:T(512)S(1)} %bitcast.122, s32[2048]{0:T(1024)S(1)} %bitcast.110, s32[512]{0:T(512)S(1)} %bitcast.120, s32[2048]{0:T(1024)S(1)} %bitcast.106, s32[512]{0:T(512)S(1)} %bitcast.118), kind=kOutput, calls=%fused_computation.27.clone.1 | convolution fusion | flops 554696704 | bytes 1603584 | tf_op jit(solution)/shard_map/while/body/eval_jaxpr/dot_general | solution.py:89
  668.8 17.8 %fusion.98 = f32[512,256]{0,1:T(8,128)S(1)} fusion(bf16[2048,256]{1,0:T(8,128)(2,1)S(1)} %get-tuple-element.285, s32[2048]{0:T(1024)S(1)} %bitcast.108, s32[512]{0:T(512)S(1)} %bitcast.122, s32[2048]{0:T(1024)S(1)} %bitcast.110, s32[512]{0:T(512)S(1)} %bitcast.120, s32[2048]{0:T(1024)S(1)} %bitcast.106, s32[512]{0:T(512)S(1)} %bitcast.118), kind=kOutput, calls=%fused_computation.27.clone.1 | convolution fusion | flops 554696704 | bytes 1603584 | tf_op jit(solution)/shard_map/while/body/eval_jaxpr/dot_general | solution.py:89
  689.4 17.7 %fusion.99 = f32[512,256]{0,1:T(8,128)S(1)} fusion(bf16[2048,256]{1,0:T(8,128)(2,1)S(1)} %get-tuple-element.285, s32[2048]{0:T(1024)S(1)} %bitcast.107, s32[512]{0:T(512)S(1)} %bitcast.121, s32[2048]{0:T(1024)S(1)} %bitcast.109, s32[512]{0:T(512)S(1)} %bitcast.119, s32[2048]{0:T(1024)S(1)} %bitcast.105, s32[512]{0:T(512)S(1)} %bitcast.117), kind=kOutput, calls=%fused_computation.26.clone.1 | convolution fusion | flops 553648128 | bytes 1603584 | tf_op jit(solution)/shard_map/while/body/eval_jaxpr/dot_general | solution.py:88
  745.1 17.8 %fusion.98 = f32[512,256]{0,1:T(8,128)S(1)} fusion(bf16[2048,256]{1,0:T(8,128)(2,1)S(1)} %get-tuple-element.285, s32[2048]{0:T(1024)S(1)} %bitcast.108, s32[512]{0:T(512)S(1)} %bitcast.122, s32[2048]{0:T(1024)S(1)} %bitcast.110, s32[512]{0:T(512)S(1)} %bitcast.120, s32[2048]{0:T(1024)S(1)} %bitcast.106, s32[512]{0:T(512)S(1)} %bitcast.118), kind=kOutput, calls=%fused_computation.27.clone.1 | convolution fusion | flops 554696704 | bytes 1603584 | tf_op jit(solution)/shard_map/while/body/eval_jaxpr/dot_general | solution.py:89
  765.6 17.7 %fusion.99 = f32[512,256]{0,1:T(8,128)S(1)} fusion(bf16[2048,256]{1,0:T(8,128)(2,1)S(1)} %get-tuple-element.285, s32[2048]{0:T(1024)S(1)} %bitcast.107, s32[512]{0:T(512)S(1)} %bitcast.121, s32[2048]{0:T(1024)S(1)} %bitcast.109, s32[512]{0:T(512)S(1)} %bitcast.119, s32[2048]{0:T(1024)S(1)} %bitcast.105, s32[512]{0:T(512)S(1)} %bitcast.117), kind=kOutput, calls=%fused_computation.26.clone.1 | convolution fusion | flops 553648128 | bytes 1603584 | tf_op jit(solution)/shard_map/while/body/eval_jaxpr/dot_general | solution.py:88
  821.3 17.8 %fusion.98 = f32[512,256]{0,1:T(8,128)S(1)} fusion(bf16[2048,256]{1,0:T(8,128)(2,1)S(1)} %get-tuple-element.285, s32[2048]{0:T(1024)S(1)} %bitcast.108, s32[512]{0:T(512)S(1)} %bitcast.122, s32[2048]{0:T(1024)S(1)} %bitcast.110, s32[512]{0:T(512)S(1)} %bitcast.120, s32[2048]{0:T(1024)S(1)} %bitcast.106, s32[512]{0:T(512)S(1)} %bitcast.118), kind=kOutput, calls=%fused_computation.27.clone.1 | convolution fusion | flops 554696704 | bytes 1603584 | tf_op jit(solution)/shard_map/while/body/eval_jaxpr/dot_general | solution.py:89
  841.8 17.7 %fusion.99 = f32[512,256]{0,1:T(8,128)S(1)} fusion(bf16[2048,256]{1,0:T(8,128)(2,1)S(1)} %get-tuple-element.285, s32[2048]{0:T(1024)S(1)} %bitcast.107, s32[512]{0:T(512)S(1)} %bitcast.121, s32[2048]{0:T(1024)S(1)} %bitcast.109, s32[512]{0:T(512)S(1)} %bitcast.119, s32[2048]{0:T(1024)S(1)} %bitcast.105, s32[512]{0:T(512)S(1)} %bitcast.117), kind=kOutput, calls=%fused_computation.26.clone.1 | convolution fusion | flops 553648128 | bytes 1603584 | tf_op jit(solution)/shard_map/while/body/eval_jaxpr/dot_general | solution.py:88
  880.8 78.8 %reduce-scatter.5.cloned.1.call-done = f32[256,256]{1,0:T(8,128)} async-done(((f32[4096,256]{1,0:T(8,128)}), f32[256,256]{1,0:T(8,128)}) %reduce-scatter.5.cloned.1.call-update) | async-done | bytes 262160 | tf_op jit(solution)/shard_map/reduce_scatter | solution.py:94
  961.3 26.6 %all_to_all.31 = bf16[128,16,256]{2,1,0:T(8,128)(2,1)S(1)} all-to-all(bf16[128,16,256]{2,1,0:T(8,128)(2,1)S(1)} %bitcast.97), channel_id=1, replica_groups=mesh['row'=8,'col'=16] {'row','col'}, dimensions={0} | all-to-all | bytes 2097152 | tf_op jit(solution)/shard_map/all_to_all | solution.py:100
  (194 shorter events, 431.0 us)
Async XLA Ops:
  8.9 55.6 %copy-start.2 = (s32[3,256]{1,0:T(4,128)S(1)}, s32[3,256]{1,0:T(4,128)}, u32[]{:S(2)}) copy-start(s32[3,256]{1,0:T(4,128)} %param.10) | copy-start | bytes 9220
  14.2 20.6 %all-to-all-start = ((s32[128,1,16]{2,1,0:T(1,128)}), s32[128,1,16]{2,1,0:T(1,128)S(1)}, u32[]{:S(2)}, u32[]{:S(2)}) async-start(s32[128,1,16]{2,1,0:T(1,128)} %bitcast.20), calls=%async_computation | async-start | bytes 131072 | tf_op jit(solution)/shard_map/all_to_all | solution.py:68
  34.8 28.0 %all-to-all-start.1 = ((bf16[128,16,256]{2,1,0:T(8,128)(2,1)}), bf16[128,16,256]{2,1,0:T(8,128)(2,1)S(1)}, u32[]{:S(2)}, u32[]{:S(2)}) async-start(bf16[128,16,256]{2,1,0:T(8,128)(2,1)} %bitcast.21), calls=%async_computation.1 | async-start | bytes 2097152 | tf_op jit(solution)/shard_map/all_to_all | solution.py:65
  43.8 55.5 %all-gather.3.cloned.1.call-start = ((), (), s32[]{:S(2)}) async-start(), calls=%async_computation.7 | async-start | bytes 1179648 | tf_op jit(solution)/shard_map/all_gather | solution.py:80
  64.5 423.9 %reduce-scatter.3.cloned.1.call-start = ((), (), s32[]{:S(2)}) async-start(), calls=%async_computation.8 | async-start | bytes 4456448 | tf_op jit(solution)/shard_map/reduce_scatter | solution.py:94
  99.2 2.3 copy-start.5
  412.4 86.3 %copy-start.3 = (f32[2]{0:T(128)S(1)}, f32[2]{0:T(128)}, u32[]{:S(2)}) copy-start(f32[2]{0:T(128)} %param.11) | copy-start | bytes 28
  412.4 107.9 %copy-start = (bf16[384,256]{1,0:T(8,128)(2,1)S(1)}, bf16[384,256]{1,0:T(8,128)(2,1)}, u32[]{:S(2)}) copy-start(bf16[384,256]{1,0:T(8,128)(2,1)} %param.8) | copy-start | bytes 589828
  490.8 26.8 %all-to-all-start.2 = ((bf16[128,16,256]{2,1,0:T(8,128)(2,1)}), bf16[128,16,256]{2,1,0:T(8,128)(2,1)S(1)}, u32[]{:S(2)}, u32[]{:S(2)}) async-start(bf16[128,16,256]{2,1,0:T(8,128)(2,1)} %bitcast.24), calls=%async_computation.3 | async-start | bytes 2097152 | tf_op jit(solution)/shard_map/all_to_all | solution.py:100
  498.6 72.5 %all-gather.5.cloned.1.call-start = ((), (), s32[]{:S(2)}) async-start(), calls=%async_computation.9 | async-start | bytes 1179648 | tf_op jit(solution)/shard_map/all_gather | solution.py:80
  552.3 407.2 %reduce-scatter.5.cloned.1.call-start = ((), (), s32[]{:S(2)}) async-start(), calls=%async_computation.10 | async-start | bytes 4456448 | tf_op jit(solution)/shard_map/reduce_scatter | solution.py:94
  571.1 2.3 copy-start.4
  960.5 31.5 %copy-start.1 = (bf16[256,256]{1,0:T(8,128)(2,1)}, bf16[256,256]{1,0:T(8,128)(2,1)S(1)}, u32[]{:S(2)}) copy-start(bf16[256,256]{1,0:T(8,128)(2,1)S(1)} %convert_element_type.89) | copy-start | bytes 393220
Sparse Core Ops, SparseCore 0:
  64.6 18.6 all-gather.2
  412.5 75.7 reduce-scatter.2
  552.5 18.5 all-gather.4
  880.9 78.6 reduce-scatter.4
where the time goes:
time: 1010 us; the launch traced here: 999 us
  matrix products  572 us (57%)
  waiting for transfers between devices  210 us (21%)
  blocking collectives  84.3 us (8%)
  local copies, waits for them, and re-layouts  45.2 us (4%)
  starting transfers between devices  28 us (3%)
  loops' own time  23.8 us (2%)
  other arithmetic  21.6 us (2%)
  between operations  14.2 us (1%)
    dot_general x16, matrix products, one_block(): jnp.dot(g_imag, piece, preferred_element_type=jnp.float32)  284 us
    dot_general x16, matrix products, one_block(): jnp.dot(g_real, piece, preferred_element_type=jnp.float32)  281 us
    reduce_scatter x2, waiting for transfers between devices, per_device(): lax.psum_scatter(partial_value, 'col', scatter_dimension=0, tiled=True)  155 us
    all_to_all x1, blocking collectives, per_device(): lax.all_to_all(flat_vals, ('row', 'col'), split_axis=0, concat_axis=0, ti...  26.6 us
    another operation x2, loops' own time, per_device(): blocks = lax.map(one_block, jnp.arange(n_blocks, dtype=jnp.int32))  23.8 us
    all_to_all x1, blocking collectives, per_device(): lax.all_to_all(route_flat_vals, ('row', 'col'), split_axis=0, concat_axis...  23 us
    all_gather x1, blocking collectives, per_device(): row_points = lax.all_gather(centroids, 'col', axis=1, tiled=True)  21.7 us
  transfers between devices with their start and end apart: 7, of which 6 were waited for; matrix products, arithmetic and copies ran while one was open for 1% of the time, Pallas kernels for 0%

commit v1 on v0

v1 whole, which is shorter than its diff:
```python
import functools

import jax
import jax.numpy as jnp
from jax import lax
from jax.experimental import pallas as pl
from jax.experimental.pallas import tpu as pltpu
from jax.sharding import PartitionSpec as P

MESH = pl.DeviceIdType.MESH
F32 = jnp.float32
BF16 = jnp.bfloat16

COS = (0.9999992, -19.73897818, 64.92858784, -85.27084363, 58.78694076, -21.06542941)
SIN = (6.28318491, -41.3415883, 81.59991362, -76.6141403, 41.34136538, -12.46881862)
AMP = 0.2 / 32.0


def iota(shape, dim):
    return lax.broadcasted_iota(jnp.int32, shape, dim)


def horner(coefs, s, scale):
    acc = jnp.float32(coefs[-1] * scale)
    for c in coefs[-2::-1]:
        acc = acc * s + jnp.float32(c * scale)
    return acc


def features(points, as_rows):
    n = points.shape[1]
    x, y, z = points[0:1], points[1:2], points[2:3]
    norm = x * x + y * y + z * z
    if as_rows:
        norm = norm + 1
    top = norm - (norm & 511)
    low = norm & 511
    mid = low - (low & 1)
    bit = low & 1
    one = jnp.ones((1, n), jnp.int32)
    if as_rows:
        rows = [x, y, z, top, mid, bit, one, one, one]
        scale = 1.0
    else:
        rows = [-2 * x, -2 * y, -2 * z, one, one, one, top, mid, bit]
        scale = 1.0 / 1024.0
    at = iota((16, n), 0)
    out = jnp.zeros((16, n), F32)
    for k, row in enumerate(rows):
        out = jnp.where(at == k, row.astype(F32) * scale, out)
    return out.astype(BF16)


def kernel(
    n_row, n_col,
    cur_ref, inc_ref, cen_ref, w_ref,
    upd_ref, pot_ref,
    tile, b_out, b_in, f_out, f_in, q_in, rs_out, rs_in, qq, place, pick,
    lab_flat, lab_out, lab_in, row_cen, col_cen, feat_row, feat_col, cur,
    send_sem, recv_sem,
):
    devices = n_row * n_col
    edge_dev, width = cur_ref.shape
    half = width // 2
    tri = cen_ref.shape[1]
    cells = b_out.shape[0]
    slots = cells // devices
    n_cols = n_row * tri
    n_sweeps = w_ref.shape[0]
    my_row, my_col = lax.axis_index("row"), lax.axis_index("col")
    me = my_row * n_col + my_col

    def flat_id(index):
        return (lax.div(index, n_col), lax.rem(index, n_col))

    def ahead(d):
        return flat_id(lax.rem(me + d, devices))

    def behind(d):
        return flat_id(lax.rem(me + devices - d, devices))

    def row_ahead(r):
        return (lax.rem(my_row + r, n_row), my_col)

    def col_ahead(t):
        return (my_row, lax.rem(my_col + t, n_col))

    def remote(src, dst, k, device):
        return pltpu.make_async_remote_copy(
            src_ref=src, dst_ref=dst, send_sem=send_sem.at[k], recv_sem=recv_sem.at[k],
            device_id=device, device_id_type=MESH,
        )

    barrier = pltpu.get_barrier_semaphore()

    def greet(d, carry):
        pl.semaphore_signal(barrier, inc=1, device_id=ahead(d), device_id_type=MESH)
        return carry

    lax.fori_loop(1, devices, greet, 0)

    both = jnp.concatenate([inc_ref[0:1, :], inc_ref[1:2, :]], axis=1)
    n_con = both.shape[1]
    owner = lax.shift_right_logical(both, tri.bit_length() - 1)
    local = (both & (tri - 1)).astype(F32)
    rel = (owner - me + devices) & (devices - 1)
    hits = jnp.where(rel == iota((devices, n_con), 0), 1.0, 0.0)
    hits16 = hits.astype(BF16)
    earlier = jnp.where(iota((n_con, n_con), 0) < iota((n_con, n_con), 1), 1.0, 0.0).astype(BF16)
    before = jnp.dot(hits16, earlier, preferred_element_type=F32)
    rank = jnp.sum(hits * before, axis=0, keepdims=True)
    slot = rel.astype(F32) * float(slots) + rank
    marks = jnp.where(rank == iota((128, n_con), 0).astype(F32), local + 1.0, 0.0).astype(BF16)
    lab_flat[...] = lax.dot_general(
        hits16, marks, (((1,), (1,)), ((), ())), preferred_element_type=F32
    )
    slot_plus, slot_minus = slot[:, :edge_dev], slot[:, edge_dev:]

    def spread(d, carry):
        lab_out[d] = lab_flat[pl.ds(d, 1), :]
        return carry

    lax.fori_loop(0, devices, spread, 0)
    chunk = 256

    def fill_place(h, carry):
        at = (iota((chunk, edge_dev), 0) + h * chunk).astype(F32)
        rows = jnp.where(slot_plus == at, 1.0, 0.0) - jnp.where(slot_minus == at, 1.0, 0.0)
        place[pl.ds(pl.multiple_of(h * chunk, chunk), chunk), :] = rows.astype(BF16)
        return carry

    lax.fori_loop(0, cells // chunk, fill_place, 0)
    cur[...] = cur_ref[...]

    def fill_out():
        def one(h, carry):
            at = pl.ds(pl.multiple_of(h * chunk, chunk), chunk)
            b_out[at, :] = jnp.dot(place[at, :], cur[...], preferred_element_type=F32).astype(BF16)
            return carry

        lax.fori_loop(0, cells // chunk, one, 0)

    fill_out()
    pl.semaphore_wait(barrier, devices - 1)

    K_ROWC, K_COLC, K_LAB = 0, 1, 2
    K_B, K_Q, K_R, K_F = 3, 3 + n_sweeps, 3 + 2 * n_sweeps, 3 + 3 * n_sweeps

    def send_row_cen(t, carry):
        to = (my_row, lax.rem(my_col + 2 * n_col - 1 - t, n_col))
        remote(cen_ref, row_cen.at[t], K_ROWC, to).start()
        return carry

    def send_col_cen(r, carry):
        remote(cen_ref, col_cen.at[r], K_COLC, row_ahead(r)).start()
        return carry

    lax.fori_loop(0, n_col - 1, send_row_cen, 0)
    lax.fori_loop(1, n_row, send_col_cen, 0)

    def block(d):
        return pl.ds(pl.multiple_of(d * slots, slots), slots)

    def send_labels(d, carry):
        remote(lab_out.at[d], lab_in.at[d], K_LAB, ahead(d)).start()
        return carry

    lax.fori_loop(1, devices, send_labels, 0)

    def send_currents(sweep):
        def one(d, carry):
            remote(b_out.at[block(d)], b_in.at[sweep, block(d)], K_B + sweep, ahead(d)).start()
            return carry

        lax.fori_loop(1, devices, one, 0)

    rest = pl.ds(slots, cells - slots)
    nobody = ahead(1)

    send_currents(0)
    b_in[0, 0:slots, :] = b_out[0:slots, :]
    lab_in[0] = lab_out[0]
    row_cen[n_col - 1] = cen_ref[...]
    col_cen[0] = cen_ref[...]

    drop_rows = pl.ds(0, n_col - 1)
    drop_cols = pl.ds(1, n_row - 1)
    row_wait = remote(row_cen.at[drop_rows], row_cen.at[drop_rows], K_ROWC, nobody)
    col_wait = remote(col_cen.at[drop_cols], col_cen.at[drop_cols], K_COLC, nobody)
    row_wait.wait_send()
    col_wait.wait_send()
    row_wait.wait_recv()
    col_wait.wait_recv()
    for t in range(n_col):
        feat_row[:, t * tri:(t + 1) * tri] = features(row_cen[t], True)
    for r in range(n_row):
        feat_col[:, r * tri:(r + 1) * tri] = features(col_cen[r], False)

    step = 128

    def make_tile(t, carry):
        at = pl.ds(pl.multiple_of(t * step, step), step)
        dist = lax.dot_general(
            feat_row[:, at], feat_col[...], (((0,), (0,)), ((), ())), preferred_element_type=F32
        )
        inv = lax.rsqrt(dist)
        turns = dist * inv
        r = turns - jnp.round(turns)
        s = r * r
        tile[at, 0:n_cols] = (inv * horner(COS, s, AMP)).astype(BF16)
        tile[at, n_cols:2 * n_cols] = ((inv * r) * horner(SIN, s, -AMP)).astype(BF16)
        return carry

    n_steps = n_col * tri // step
    first = n_steps * 5 // 8
    lax.fori_loop(0, first, make_tile, 0)

    def charges_of(sweep):
        wait = remote(b_out.at[rest], b_in.at[sweep, rest], K_B + sweep, nobody)
        wait.wait_recv()
        if sweep == 0:
            labels = remote(lab_out.at[pl.ds(1, devices - 1)], lab_in.at[pl.ds(1, devices - 1)], K_LAB, nobody)
            labels.wait_send()
            labels.wait_recv()

            def gather(d, carry):
                lab_flat[pl.ds(d, 1), :] = lab_in[d]
                return carry

            lax.fori_loop(0, devices, gather, 0)
            group = chunk // slots
            widen = jnp.where(
                lax.div(iota((chunk, group), 0), slots) == iota((chunk, group), 1), 1.0, 0.0
            ).astype(BF16)
            keep = jnp.where(
                lax.rem(iota((chunk, 128), 0), slots) == iota((chunk, 128), 1), 1.0, 0.0
            )
            ones = jnp.ones((128, tri), BF16)
            target = (iota((chunk, tri), 1) + 1).astype(F32)

            def fill_pick(h, carry):
                here = lab_flat[pl.ds(pl.multiple_of(h * group, group), group), :].astype(BF16)
                wide = jnp.dot(widen, here, preferred_element_type=F32) * keep
                label = jnp.dot(wide.astype(BF16), ones, preferred_element_type=F32)
                pick[pl.ds(pl.multiple_of(h * chunk, chunk), chunk), :] = jnp.where(
                    label == target, 1.0, 0.0
                ).astype(BF16)
                return carry

            lax.fori_loop(0, cells // chunk, fill_pick, 0)
        charges = lax.dot_general(
            pick[...], b_in[sweep], (((0,), (0,)), ((), ())), preferred_element_type=F32
        ).astype(BF16)
        q_in[sweep, 0:tri, :] = charges

        def send(r, carry):
            remote(
                q_in.at[sweep, pl.ds(0, tri)],
                q_in.at[sweep, pl.ds(pl.multiple_of(r * tri, tri), tri)],
                K_Q + sweep, row_ahead(r),
            ).start()
            return carry

        lax.fori_loop(1, n_row, send, 0)
        wait.wait_send()

    for sweep in range(n_sweeps):
        charges_of(sweep)
        if sweep == 0:
            lax.fori_loop(first, n_steps, make_tile, 0)
        others = pl.ds(tri, n_cols - tri)
        q_wait = remote(q_in.at[sweep, others], q_in.at[sweep, others], K_Q + sweep, nobody)
        q_wait.wait_recv()

        def fill_qq(r, carry):
            at = pl.ds(pl.multiple_of(r * tri, tri), tri)
            below = pl.ds(pl.multiple_of(n_cols + r * tri, tri), tri)
            q = q_in[sweep, at, :]
            qq[at, :] = q
            qq[below, 0:half] = -q[:, half:]
            qq[below, half:] = q[:, :half]
            return carry

        lax.fori_loop(0, n_row, fill_qq, 0)

        def partial(t):
            at = pl.ds(pl.multiple_of(t * tri, tri), tri)
            return jnp.dot(tile[at, :], qq[...], preferred_element_type=F32)

        def one_owner(t, carry):
            rs_out[t] = partial(t).astype(BF16)
            remote(rs_out.at[t], rs_in.at[sweep, t], K_R + sweep, col_ahead(t + 1)).start()
            return carry

        lax.fori_loop(0, n_col - 1, one_owner, 0)
        total = partial(n_col - 1)
        pieces = pl.ds(0, n_col - 1)
        r_wait = remote(rs_out.at[pieces], rs_in.at[sweep, pieces], K_R + sweep, nobody)
        r_wait.wait_recv()
        q_wait.wait_send()
        for t in range(n_col - 1):
            total = total + rs_in[sweep, t].astype(F32)
        potential = total.astype(BF16)
        if sweep == n_sweeps - 1:
            pot_ref[...] = potential

        def fill_answers(h, carry):
            at = pl.ds(pl.multiple_of(h * chunk, chunk), chunk)
            f_out[at, :] = jnp.dot(pick[at, :], potential, preferred_element_type=F32).astype(BF16)
            return carry

        lax.fori_loop(0, cells // chunk, fill_answers, 0)

        def send_back(d, carry):
            remote(f_out.at[block(d)], f_in.at[sweep, block(d)], K_F + sweep, behind(d)).start()
            return carry

        lax.fori_loop(1, devices, send_back, 0)
        f_in[sweep, 0:slots, :] = f_out[0:slots, :]
        f_wait = remote(f_out.at[rest], f_in.at[sweep, rest], K_F + sweep, nobody)
        r_wait.wait_send()
        f_wait.wait_recv()
        slope = lax.dot_general(
            place[...], f_in[sweep], (((0,), (0,)), ((), ())), preferred_element_type=F32
        )
        updated = (cur[...].astype(F32) - w_ref[sweep] * slope).astype(BF16)
        if sweep == n_sweeps - 1:
            upd_ref[...] = updated
        else:
            cur[...] = updated
            fill_out()
            send_currents(sweep + 1)
            b_in[sweep + 1, 0:slots, :] = b_out[0:slots, :]
        f_wait.wait_send()


def solution(mesh):
    n_row, n_col = mesh.shape["row"], mesh.shape["col"]
    devices = n_row * n_col

    def per_device(currents, incidence, centroids, sweep_weights):
        edge_dev, width = currents.shape
        tri = centroids.shape[1]
        n_sweeps = sweep_weights.shape[0]
        slots = 16
        cells = devices * slots
        vm = pltpu.VMEM
        return pl.pallas_call(
            functools.partial(kernel, n_row, n_col),
            out_shape=(
                jax.ShapeDtypeStruct((edge_dev, width), BF16),
                jax.ShapeDtypeStruct((tri, width), BF16),
            ),
            in_specs=[pl.BlockSpec(memory_space=pltpu.VMEM)] * 3
            + [pl.BlockSpec(memory_space=pltpu.SMEM)],
            out_specs=(pl.BlockSpec(memory_space=pltpu.VMEM),) * 2,
            scratch_shapes=[
                vm((n_col * tri, 2 * n_row * tri), BF16),
                vm((cells, width), BF16),
                vm((n_sweeps, cells, width), BF16),
                vm((cells, width), BF16),
                vm((n_sweeps, cells, width), BF16),
                vm((n_sweeps, n_row * tri, width), BF16),
                vm((n_col - 1, tri, width), BF16),
                vm((n_sweeps, n_col - 1, tri, width), BF16),
                vm((2 * n_row * tri, width), BF16),
                vm((cells, edge_dev), BF16),
                vm((cells, tri), BF16),
                vm((devices, 128), F32),
                vm((devices, 1, 128), F32),
                vm((devices, 1, 128), F32),
                vm((n_col, 3, tri), jnp.int32),
                vm((n_row, 3, tri), jnp.int32),
                vm((16, n_col * tri), BF16),
                vm((16, n_row * tri), BF16),
                vm((edge_dev, width), BF16),
                pltpu.SemaphoreType.DMA((3 + 4 * n_sweeps,)),
                pltpu.SemaphoreType.DMA((3 + 4 * n_sweeps,)),
            ],
            compiler_params=pltpu.CompilerParams(
                collective_id=0, has_side_effects=True, vmem_limit_bytes=66000000
            ),
            name="sweeps",
        )(currents, incidence, centroids, sweep_weights)

    in_specs = (P(("row", "col"), None), P(None, ("row", "col")), P(None, ("row", "col")), P())
    out_specs = (P(("row", "col"), None), P(("row", "col"), None))
    return jax.shard_map(
        per_device, mesh=mesh, in_specs=in_specs, out_specs=out_specs, check_vma=False
    )
```

time: 1010 us -> 191 us (0.19); the launches traced: 999 us -> 191 us
  matrix products: 572 us -> 0 us
  waiting for transfers between devices: 210 us -> 0 us
  Pallas kernels: 0 us -> 188 us
  blocking collectives: 84.3 us -> 0 us
  local copies, waits for them, and re-layouts: 45.2 us -> 2.31 us
  starting transfers between devices: 28 us -> 0 us
  loops' own time: 23.8 us -> 0 us
  other arithmetic: 21.6 us -> 0 us
  between operations: 14.2 us -> 0.65 us
    dot_general x36 -> x0, matrix products: 572 us -> none  [the longest x16 284 us: one_block(): jnp.dot(g_imag, piece, preferred_element_type=jnp.float32)]
    pallas_call x0 -> x1, Pallas kernels: none -> 188 us  [per_device(): pl.pallas_call(functools.partial(kernel, n_row, n_col), out_shape=(jax.Sh...]
    reduce_scatter x2 -> x0, waiting for transfers between devices: 155 us -> none  [per_device(): lax.psum_scatter(partial_value, 'col', scatter_dimension=0, tiled=True)]
    all_to_all x2 -> x0, blocking collectives: 49.6 us -> none  [the longest x1 26.6 us: per_device(): lax.all_to_all(flat_vals, ('row', 'col'), split_axis=0, concat_axis=0, ti...]
    all_to_all x3 -> x0, waiting for transfers between devices: 36.7 us -> none  [the longest x1 18.3 us: per_device(): lax.all_to_all(flat_vals, ('row', 'col'), split_axis=0, concat_axis=0, ti...]
    all_gather x2 -> x0, blocking collectives: 34.6 us -> none  [the longest x1 21.7 us: per_device(): row_points = lax.all_gather(centroids, 'col', axis=1, tiled=True)]
    all_to_all x3 -> x0, starting transfers between devices: 27.8 us -> none  [the longest x1 11.2 us: per_device(): lax.all_to_all(flat_marks, ('row', 'col'), split_axis=0, concat_axis=0, t...]
    another operation x2 -> x0, loops' own time: 23.8 us -> none  [per_device(): blocks = lax.map(one_block, jnp.arange(n_blocks, dtype=jnp.int32))]
  transfers between devices with their start and end apart: 7 -> 0, of which waited for: 6 -> 0; matrix products, arithmetic and copies ran while one was open for 1% -> 0% of each run, Pallas kernels for 0% -> 0%
where the time goes in v1:
time: 191 us
  Pallas kernels  188 us (98%)
  local copies, waits for them, and re-layouts  2.31 us (1%)
    pallas_call x1, Pallas kernels, per_device(): pl.pallas_call(functools.partial(kernel, n_row, n_col), out_shape=(jax.Sh...  188 us

profile of v1, /device:TPU:0, one launch (start us, length us, event | category | flops | bytes accessed | tf_op | source)
XLA Modules:
  0.0 191.2 jit_solution(15074889918318475053)
XLA Ops:
  0.6 188.2 %sweeps.1 = (bf16[384,256]{1,0:T(8,128)(2,1)}, bf16[256,256]{1,0:T(8,128)(2,1)}) custom-call(bf16[384,256]{1,0:T(8,128)(2,1)} %cur_ref.1, s32[2,384]{1,0:T(2,128)} %inc_ref.1, s32[3,256]{1,0:T(4,128)} %cen_ref.1, f32[2]{0:T(128)} %w_ref.1), custom_call_target="tpu_custom_call" | custom-call | tf_op jit(solution)/shard_map/sweeps/pallas_call | solution.py:348
  188.9 0.0 copy-start
  188.9 1.7 copy.8
  190.5 0.0 copy-done
  190.5 0.7 copy.9
Async XLA Ops:
  188.9 1.7 copy-start

commit v2 on v1

v2 whole, which is shorter than its diff:
```python
import functools

import jax
import jax.numpy as jnp
from jax import lax
from jax.experimental import pallas as pl
from jax.experimental.pallas import tpu as pltpu
from jax.sharding import PartitionSpec as P

MESH = pl.DeviceIdType.MESH
F32 = jnp.float32
BF16 = jnp.bfloat16

AMP = 0.2 / 32.0
ROOT = (2.0 * AMP) ** 0.5
SIN = (3.14158202, -5.1671428, 2.54189902, -0.554636165)
COS = (0.999999953, -4.93479286, 4.05841191, -1.33188016, 0.219696799)


def iota(shape, dim):
    return lax.broadcasted_iota(jnp.int32, shape, dim)


def horner(coefs, s, scale):
    acc = jnp.float32(coefs[-1] * scale)
    for c in coefs[-2::-1]:
        acc = acc * s + jnp.float32(c * scale)
    return acc


def features(points, as_rows):
    n = points.shape[1]
    x, y, z = points[0:1], points[1:2], points[2:3]
    norm = x * x + y * y + z * z
    if as_rows:
        norm = norm + 1
    top = norm - (norm & 511)
    low = norm & 511
    mid = low - (low & 1)
    bit = low & 1
    one = jnp.ones((1, n), jnp.int32)
    if as_rows:
        rows = [x, y, z, top, mid, bit, one, one, one]
        scale = 1.0
    else:
        rows = [-2 * x, -2 * y, -2 * z, one, one, one, top, mid, bit]
        scale = 1.0 / 1024.0
    at = iota((16, n), 0)
    out = jnp.zeros((16, n), F32)
    for k, row in enumerate(rows):
        out = jnp.where(at == k, row.astype(F32) * scale, out)
    return out.astype(BF16)


def kernel(
    n_row, n_col,
    cur_ref, inc_ref, cen_ref, w_ref,
    upd_ref, pot_ref,
    tile_a, tile_b, b_out, b_in, f_out, f_in, q_in, qq, place, pick,
    rs_a, rs_b, own_a, own_b, p1a, p1b, rs2a, rs2b, p2a, p2b,
    lab_flat, lab_out, lab_in, row_cen, col_cen, feat_row, feat_col, cur, pot,
    send_sem, recv_sem,
):
    devices = n_row * n_col
    edge_dev, width = cur_ref.shape
    half = width // 2
    tri = cen_ref.shape[1]
    cells = b_out.shape[0]
    slots = cells // devices
    n_cols = n_row * tri
    n_sweeps = w_ref.shape[0]
    side = 4
    my_row, my_col = lax.axis_index("row"), lax.axis_index("col")
    me = my_row * n_col + my_col
    mx, mc = lax.div(my_row, 2), lax.rem(my_row, 2)
    mz, my = lax.div(my_col, side), lax.rem(my_col, side)

    def flat_id(index):
        return (lax.div(index, n_col), lax.rem(index, n_col))

    def ahead(d):
        return flat_id(lax.rem(me + d, devices))

    def behind(d):
        return flat_id(lax.rem(me + devices - d, devices))

    def along_row(dx, dc):
        return (lax.rem(mx + dx, side) * 2 + lax.rem(mc + dc, 2), my_col)

    def along_col(dz, dy):
        return (my_row, lax.rem(mz + dz, side) * side + lax.rem(my + dy, side))

    sends, recvs = [0], [0]

    def new(count, many):
        count[0] += many
        return count[0] - many

    S_ROWC, S_COLC, S_LAB = (new(sends, 1) for _ in range(3))
    R_ROWC, R_COLC, R_LAB = (new(recvs, 1) for _ in range(3))
    S_B, S_Q, S_A1, S_B1, S_A2, S_B2, S_F = (new(sends, n_sweeps) for _ in range(7))
    R_B, R_Q2, R_B1, R_A2, R_B2, R_F = (new(recvs, n_sweeps) for _ in range(6))
    R_Q1, R_A1 = (new(recvs, n_sweeps * side) for _ in range(2))

    def remote(src, dst, s, r, device):
        return pltpu.make_async_remote_copy(
            src_ref=src, dst_ref=dst, send_sem=send_sem.at[s], recv_sem=recv_sem.at[r],
            device_id=device, device_id_type=MESH,
        )

    barrier = pltpu.get_barrier_semaphore()

    def greet(d, carry):
        pl.semaphore_signal(barrier, inc=1, device_id=ahead(devices - d), device_id_type=MESH)
        return carry

    lax.fori_loop(1, devices, greet, 0)

    both = jnp.concatenate([inc_ref[0:1, :], inc_ref[1:2, :]], axis=1)
    n_con = both.shape[1]
    owner = lax.shift_right_logical(both, tri.bit_length() - 1)
    local = (both & (tri - 1)).astype(F32)
    rel = (owner - me + devices) & (devices - 1)
    hits = jnp.where(rel == iota((devices, n_con), 0), 1.0, 0.0)
    hits16 = hits.astype(BF16)
    earlier = jnp.where(iota((n_con, n_con), 0) < iota((n_con, n_con), 1), 1.0, 0.0).astype(BF16)
    before = jnp.dot(hits16, earlier, preferred_element_type=F32)
    rank = jnp.sum(hits * before, axis=0, keepdims=True)
    slot = rel.astype(F32) * float(slots) + rank
    marks = jnp.where(rank == iota((128, n_con), 0).astype(F32), local + 1.0, 0.0).astype(BF16)
    lab_flat[...] = lax.dot_general(
        hits16, marks, (((1,), (1,)), ((), ())), preferred_element_type=F32
    )
    slot_plus, slot_minus = slot[:, :edge_dev], slot[:, edge_dev:]

    def spread(d, carry):
        lab_out[d] = lab_flat[pl.ds(d, 1), :]
        return carry

    lax.fori_loop(0, devices, spread, 0)
    chunk = 256
    group = chunk // slots
    cur[...] = cur_ref[...]

    def part(h, size):
        return pl.ds(pl.multiple_of(h * size, size), size)

    def block(d):
        return part(d, slots)

    rest = pl.ds(slots, cells - slots)
    nobody = ahead(1)

    def fill_place(h, carry):
        at = (iota((chunk, edge_dev), 0) + h * chunk).astype(F32)
        rows = jnp.where(slot_plus == at, 1.0, 0.0) - jnp.where(slot_minus == at, 1.0, 0.0)
        place[part(h, chunk), :] = rows.astype(BF16)
        return carry

    lax.fori_loop(0, cells // chunk, fill_place, 0)

    def fill_out(h):
        at = part(h, chunk)
        b_out[at, :] = jnp.dot(place[at, :], cur[...], preferred_element_type=F32).astype(BF16)

    def send_out(sweep, h):
        def one(j, carry):
            d = h * group + j

            @pl.when(d > 0)
            def _():
                remote(b_out.at[block(d)], b_in.at[sweep, block(d)], S_B + sweep, R_B + sweep, ahead(d)).start()

            return carry

        lax.fori_loop(0, group, one, 0)

    def fill_first(h, carry):
        fill_out(h)
        return carry

    lax.fori_loop(0, cells // chunk, fill_first, 0)
    pl.semaphore_wait(barrier, devices - 1)

    def send_row_cen(k, carry):
        to = along_col(lax.div(k, side) + 1, lax.rem(k, side) + 1)
        remote(cen_ref, row_cen.at[k], S_ROWC, R_ROWC, to).start()
        return carry

    def send_col_cen(r, carry):
        to = along_row(lax.rem(r, side), lax.div(r, side))
        remote(cen_ref, col_cen.at[r], S_COLC, R_COLC, to).start()
        return carry

    lax.fori_loop(1, n_row, send_col_cen, 0)
    lax.fori_loop(0, n_col - 1, send_row_cen, 0)

    def send_labels(d, carry):
        remote(lab_out.at[d], lab_in.at[d], S_LAB, R_LAB, ahead(d)).start()
        return carry

    lax.fori_loop(1, devices, send_labels, 0)

    def send_first(h, carry):
        send_out(0, h)
        return carry

    lax.fori_loop(0, cells // chunk, send_first, 0)
    b_in[0, 0:slots, :] = b_out[0:slots, :]
    lab_in[0] = lab_out[0]
    row_cen[n_col - 1] = cen_ref[...]
    col_cen[0] = cen_ref[...]

    drop_rows = pl.ds(0, n_col - 1)
    drop_cols = pl.ds(1, n_row - 1)
    row_wait = remote(row_cen.at[drop_rows], row_cen.at[drop_rows], S_ROWC, R_ROWC, nobody)
    col_wait = remote(col_cen.at[drop_cols], col_cen.at[drop_cols], S_COLC, R_COLC, nobody)
    col_wait.wait_send()
    col_wait.wait_recv()
    for r in range(n_row):
        feat_col[:, r * tri:(r + 1) * tri] = features(col_cen[r], False)
    row_wait.wait_send()
    row_wait.wait_recv()
    for t in range(n_col):
        feat_row[:, t * tri:(t + 1) * tri] = features(row_cen[t], True)

    step = 128

    def make_tile(tile, k, base):
        for u in range(tri // step):
            at = pl.ds(pl.multiple_of(k * tri + u * step, step), step)
            here = pl.ds(pl.multiple_of((k - base) * tri + u * step, step), step)
            dist = lax.dot_general(
                feat_row[:, at], feat_col[...], (((0,), (0,)), ((), ())), preferred_element_type=F32
            )
            inv = lax.rsqrt(dist)
            turns = dist * inv
            r = turns - jnp.round(turns)
            s = r * r
            sine = r * horner(SIN, s, ROOT)
            cosine = horner(COS, s, -ROOT)
            tile[here, 0:n_cols] = (inv * (jnp.float32(AMP) - sine * sine)).astype(BF16)
            tile[here, n_cols:2 * n_cols] = (inv * (sine * cosine)).astype(BF16)

    def make_a(k, carry):
        make_tile(tile_a, k, 0)
        return carry

    n_a = n_col // 2
    cut1, cut2 = 5, 7
    lax.fori_loop(0, cut1, make_a, 0)

    def fill_qq(sweep, r):
        at = pl.ds(r * tri, tri)
        below = pl.ds(n_cols + r * tri, tri)
        q = q_in[sweep, at, :]
        qq[at, :] = q
        qq[below, 0:half] = -q[:, half:]
        qq[below, half:] = q[:, :half]

    def charges_of(sweep):
        wait = remote(b_out.at[rest], b_in.at[sweep, rest], S_B + sweep, R_B + sweep, nobody)
        if sweep == 0:
            labels = remote(
                lab_out.at[pl.ds(1, devices - 1)], lab_in.at[pl.ds(1, devices - 1)], S_LAB, R_LAB, nobody
            )
            labels.wait_send()
            labels.wait_recv()

            def gather(d, carry):
                lab_flat[pl.ds(d, 1), :] = lab_in[d]
                return carry

            lax.fori_loop(0, devices, gather, 0)
            widen = jnp.where(
                lax.div(iota((chunk, group), 0), slots) == iota((chunk, group), 1), 1.0, 0.0
            ).astype(BF16)
            keep = jnp.where(
                lax.rem(iota((chunk, 128), 0), slots) == iota((chunk, 128), 1), 1.0, 0.0
            )
            ones = jnp.ones((128, tri), BF16)
            target = (iota((chunk, tri), 1) + 1).astype(F32)

            def fill_pick(h, carry):
                here = lab_flat[part(h, group), :].astype(BF16)
                wide = jnp.dot(widen, here, preferred_element_type=F32) * keep
                label = jnp.dot(wide.astype(BF16), ones, preferred_element_type=F32)
                pick[part(h, chunk), :] = jnp.where(label == target, 1.0, 0.0).astype(BF16)
                return carry

            lax.fori_loop(0, cells // chunk, fill_pick, 0)
        wait.wait_recv()
        charges = lax.dot_general(
            pick[...], b_in[sweep], (((0,), (0,)), ((), ())), preferred_element_type=F32
        ).astype(BF16)
        q_in[sweep, 0:tri, :] = charges
        mine = q_in.at[sweep, pl.ds(0, tri)]
        partner = along_row(0, 1)
        for dx in (2, 1, 3):
            remote(
                mine, q_in.at[sweep, pl.ds(dx * tri, tri)],
                S_Q + sweep, R_Q1 + sweep * side + dx, along_row(dx, 0),
            ).start()
        remote(mine, q_in.at[sweep, pl.ds(side * tri, tri)], S_Q + sweep, R_Q2 + sweep, partner).start()
        fill_qq(sweep, 0)
        if sweep == 0:
            lax.fori_loop(cut1, cut2, make_a, 0)
        for dx in (1, 3, 2):
            got = q_in.at[sweep, pl.ds(dx * tri, tri)]
            remote(got, got, S_Q + sweep, R_Q1 + sweep * side + dx, partner).wait_recv()
            remote(
                got, q_in.at[sweep, pl.ds((side + dx) * tri, tri)],
                S_Q + sweep, R_Q2 + sweep, partner,
            ).start()
            fill_qq(sweep, dx)
        if sweep == 0:
            lax.fori_loop(cut2, n_a, make_a, 0)
        far = q_in.at[sweep, pl.ds(side * tri, side * tri)]
        remote(far, far, S_Q + sweep, R_Q2 + sweep, nobody).wait_recv()
        for r in range(side, 2 * side):
            fill_qq(sweep, r)
        wait.wait_send()
        sent = q_in.at[sweep, pl.ds(tri, n_cols - tri)]
        remote(sent, sent, S_Q + sweep, R_Q2 + sweep, nobody).wait_send()

    def wait_for(ref, s, r):
        return remote(ref, ref, s, r, nobody)

    last = side - 1

    def finish_a(sweep, g):
        wait_for(p1a.at[sweep, g], S_A1 + sweep, R_A1 + sweep * side + g).wait_recv()
        total = own_a[g]
        for j in range(last):
            total = total + p1a[sweep, g, j].astype(F32)
        return total

    def finish_b(sweep, g):
        total = own_b[g]
        for j in range(last):
            total = total + p1b[sweep, j, g].astype(F32)
        return total

    def emit(sweep, k, value):
        gz, gy = lax.div(k, side), lax.rem(k, side)
        left, right = value[:, :half], value[:, half:]

        @pl.when(gy < last)
        def _():
            rs_a[k] = left.astype(BF16)
            remote(
                rs_a.at[k], p1a.at[sweep, gz, gy], S_A1 + sweep, R_A1 + sweep * side + gz,
                along_col(0, last - gy),
            ).start()

        @pl.when(gz < last)
        def _():
            rs_b[k] = right.astype(BF16)
            remote(
                rs_b.at[k], p1b.at[sweep, gz, gy], S_B1 + sweep, R_B1 + sweep,
                along_col(last - gz, 0),
            ).start()

        @pl.when(gy == last)
        def _():
            own_a[gz] = left

        @pl.when(gz == last)
        def _():
            own_b[gy] = right

        @pl.when(jnp.logical_and(gy == last, gz > 0))
        def _():
            g = gz - 1
            rs2a[g] = finish_a(sweep, g).astype(BF16)
            remote(
                rs2a.at[g], p2a.at[sweep, g], S_A2 + sweep, R_A2 + sweep, along_col(last - g, 0)
            ).start()

    for sweep in range(n_sweeps):
        charges_of(sweep)

        def upper(k, carry):
            value = jnp.dot(tile_a[part(k, tri), :], qq[...], preferred_element_type=F32)
            if sweep == 0:
                make_tile(tile_b, k + n_a, n_a)
            emit(sweep, k, value)
            return carry

        def lower(k, carry):
            value = jnp.dot(tile_b[part(k - n_a, tri), :], qq[...], preferred_element_type=F32)
            emit(sweep, k, value)
            return carry

        lax.fori_loop(0, n_a, upper, 0)
        lax.fori_loop(n_a, n_col, lower, 0)
        wait_for(p1b.at[sweep], S_B1 + sweep, R_B1 + sweep).wait_recv()
        for g in range(last):
            rs2b[g] = finish_b(sweep, g).astype(BF16)
            remote(
                rs2b.at[g], p2b.at[sweep, g], S_B2 + sweep, R_B2 + sweep, along_col(0, last - g)
            ).start()
        left = finish_a(sweep, last)
        right = finish_b(sweep, last)
        wait_for(p2a.at[sweep], S_A2 + sweep, R_A2 + sweep).wait_recv()
        for j in range(last):
            left = left + p2a[sweep, j].astype(F32)
        pot[:, :half] = left.astype(BF16)
        wait_for(p2b.at[sweep], S_B2 + sweep, R_B2 + sweep).wait_recv()
        for j in range(last):
            right = right + p2b[sweep, j].astype(F32)
        pot[:, half:] = right.astype(BF16)

        def answer(h, carry):
            at = part(h, chunk)
            f_out[at, :] = jnp.dot(pick[at, :], pot[...], preferred_element_type=F32).astype(BF16)

            def send_back(j, carry):
                d = h * group + j

                @pl.when(d > 0)
                def _():
                    remote(
                        f_out.at[block(d)], f_in.at[sweep, block(d)], S_F + sweep, R_F + sweep, behind(d)
                    ).start()

                return carry

            lax.fori_loop(0, group, send_back, 0)
            return carry

        lax.fori_loop(0, cells // chunk, answer, 0)
        f_in[sweep, 0:slots, :] = f_out[0:slots, :]
        if sweep == n_sweeps - 1:
            pot_ref[...] = pot[...]
        f_wait = remote(f_out.at[rest], f_in.at[sweep, rest], S_F + sweep, R_F + sweep, nobody)
        wait_for(rs_a.at[pl.ds(0, last * side)], S_A1 + sweep, R_B1 + sweep).wait_send()
        wait_for(rs_b.at[pl.ds(0, last * side)], S_B1 + sweep, R_B1 + sweep).wait_send()
        wait_for(rs2a, S_A2 + sweep, R_A2 + sweep).wait_send()
        wait_for(rs2b, S_B2 + sweep, R_B2 + sweep).wait_send()
        f_wait.wait_recv()
        slope = lax.dot_general(
            place[...], f_in[sweep], (((0,), (0,)), ((), ())), preferred_element_type=F32
        )
        updated = (cur[...].astype(F32) - w_ref[sweep] * slope).astype(BF16)
        if sweep == n_sweeps - 1:
            upd_ref[...] = updated
        else:
            cur[...] = updated

            def next_out(h, carry):
                fill_out(h)
                send_out(sweep + 1, h)
                return carry

            lax.fori_loop(0, cells // chunk, next_out, 0)
            b_in[sweep + 1, 0:slots, :] = b_out[0:slots, :]
        f_wait.wait_send()


def solution(mesh):
    n_row, n_col = mesh.shape["row"], mesh.shape["col"]
    devices = n_row * n_col

    def per_device(currents, incidence, centroids, sweep_weights):
        edge_dev, width = currents.shape
        tri = centroids.shape[1]
        n_sweeps = sweep_weights.shape[0]
        slots = 16
        cells = devices * slots
        vm = pltpu.VMEM
        return pl.pallas_call(
            functools.partial(kernel, n_row, n_col),
            out_shape=(
                jax.ShapeDtypeStruct((edge_dev, width), BF16),
                jax.ShapeDtypeStruct((tri, width), BF16),
            ),
            in_specs=[pl.BlockSpec(memory_space=pltpu.VMEM)] * 3
            + [pl.BlockSpec(memory_space=pltpu.SMEM)],
            out_specs=(pl.BlockSpec(memory_space=pltpu.VMEM),) * 2,
            scratch_shapes=[
                vm((n_col * tri // 2, 2 * n_row * tri), BF16),
                vm((n_col * tri // 2, 2 * n_row * tri), BF16),
                vm((cells, width), BF16),
                vm((n_sweeps, cells, width), BF16),
                vm((cells, width), BF16),
                vm((n_sweeps, cells, width), BF16),
                vm((n_sweeps, n_row * tri, width), BF16),
                vm((2 * n_row * tri, width), BF16),
                vm((cells, edge_dev), BF16),
                vm((cells, tri), BF16),
                vm((n_col, tri, width // 2), BF16),
                vm((n_col, tri, width // 2), BF16),
                vm((4, tri, width // 2), F32),
                vm((4, tri, width // 2), F32),
                vm((n_sweeps, 4, 3, tri, width // 2), BF16),
                vm((n_sweeps, 3, 4, tri, width // 2), BF16),
                vm((3, tri, width // 2), BF16),
                vm((3, tri, width // 2), BF16),
                vm((n_sweeps, 3, tri, width // 2), BF16),
                vm((n_sweeps, 3, tri, width // 2), BF16),
                vm((devices, 128), F32),
                vm((devices, 1, 128), F32),
                vm((devices, 1, 128), F32),
                vm((n_col, 3, tri), jnp.int32),
                vm((n_row, 3, tri), jnp.int32),
                vm((16, n_col * tri), BF16),
                vm((16, n_row * tri), BF16),
                vm((edge_dev, width), BF16),
                vm((tri, width), BF16),
                pltpu.SemaphoreType.DMA((3 + 7 * n_sweeps,)),
                pltpu.SemaphoreType.DMA((3 + 14 * n_sweeps,)),
            ],
            compiler_params=pltpu.CompilerParams(
                collective_id=0, has_side_effects=True, vmem_limit_bytes=66000000
            ),
            name="sweeps",
        )(currents, incidence, centroids, sweep_weights)

    in_specs = (P(("row", "col"), None), P(None, ("row", "col")), P(None, ("row", "col")), P())
    out_specs = (P(("row", "col"), None), P(("row", "col"), None))
    return jax.shard_map(
        per_device, mesh=mesh, in_specs=in_specs, out_specs=out_specs, check_vma=False
    )
```

time: 191 us -> 157 us (0.82)
  Pallas kernels: 188 us -> 154 us
    pallas_call x1, Pallas kernels: 188 us -> 154 us  [per_device(): pl.pallas_call(functools.partial(kernel, n_row, n_col), out_shape=(jax.Sh...]
where the time goes in v2:
time: 157 us
  Pallas kernels  154 us (98%)
  local copies, waits for them, and re-layouts  2.31 us (1%)
    pallas_call x1, Pallas kernels, per_device(): pl.pallas_call(functools.partial(kernel, n_row, n_col), out_shape=(jax.Sh...  154 us

profile of v2, /device:TPU:0, one launch (start us, length us, event | category | flops | bytes accessed | tf_op | source)
XLA Modules:
  0.0 157.1 jit_solution(11704757589248437814)
XLA Ops:
  0.6 154.1 %sweeps.1 = (bf16[384,256]{1,0:T(8,128)(2,1)}, bf16[256,256]{1,0:T(8,128)(2,1)}) custom-call(bf16[384,256]{1,0:T(8,128)(2,1)} %cur_ref.1, s32[2,384]{1,0:T(2,128)} %inc_ref.1, s32[3,256]{1,0:T(4,128)} %cen_ref.1, f32[2]{0:T(128)} %w_ref.1), custom_call_target="tpu_custom_call" | custom-call | tf_op jit(solution)/shard_map/sweeps/pallas_call | solution.py:472
  154.7 0.0 copy-start
  154.7 1.7 %copy.8 = bf16[384,256]{1,0:T(8,128)(2,1)} copy(bf16[384,256]{1,0:T(8,128)(2,1)} %get-tuple-element.4) | data formatting | bytes 393216
  156.4 0.0 copy-done
  156.4 0.7 copy.9
Async XLA Ops:
  154.7 1.7 %copy-start = (bf16[256,256]{1,0:T(8,128)(2,1)S(1)}, bf16[256,256]{1,0:T(8,128)(2,1)}, u32[]{:S(2)}) copy-start(bf16[256,256]{1,0:T(8,128)(2,1)} %get-tuple-element.5) | copy-start | bytes 393220

commit v3 on v2

v3 whole, which is shorter than its diff:
```python
import functools

import jax
import jax.numpy as jnp
from jax import lax
from jax.experimental import pallas as pl
from jax.experimental.pallas import tpu as pltpu
from jax.sharding import PartitionSpec as P

MESH = pl.DeviceIdType.MESH
F32 = jnp.float32
BF16 = jnp.bfloat16

AMP = 0.2 / 32.0
ROOT = (2.0 * AMP) ** 0.5
SIN = (3.14158202, -5.1671428, 2.54189902, -0.554636165)
COS = (0.999999953, -4.93479286, 4.05841191, -1.33188016, 0.219696799)


def iota(shape, dim):
    return lax.broadcasted_iota(jnp.int32, shape, dim)


def horner(coefs, s, scale):
    acc = jnp.float32(coefs[-1] * scale)
    for c in coefs[-2::-1]:
        acc = acc * s + jnp.float32(c * scale)
    return acc


def features(points, as_rows):
    n = points.shape[1]
    x, y, z = points[0:1], points[1:2], points[2:3]
    norm = x * x + y * y + z * z
    if as_rows:
        norm = norm + 1
    top = norm - (norm & 511)
    low = norm & 511
    mid = low - (low & 1)
    bit = low & 1
    one = jnp.ones((1, n), jnp.int32)
    if as_rows:
        rows = [x, y, z, top, mid, bit, one, one, one]
        scale = 1.0
    else:
        rows = [-2 * x, -2 * y, -2 * z, one, one, one, top, mid, bit]
        scale = 1.0 / 1024.0
    at = iota((16, n), 0)
    out = jnp.zeros((16, n), F32)
    for k, row in enumerate(rows):
        out = jnp.where(at == k, row.astype(F32) * scale, out)
    return out.astype(BF16)


def kernel(
    n_row, n_col,
    cur_ref, inc_ref, cen_ref, w_ref,
    upd_ref, pot_ref,
    tile_a, tile_b, b_out, b_in, f_out, f_in, q_in, qq, place, place_t, pick, pick_t,
    rs_a, rs_b, own_a, own_b, p1a, p1b, rs2a, rs2b, p2a, p2b,
    lab_flat, lab_out, lab_in, row_cen, col_cen, feat_row, feat_col, cur, pot,
    send_sem, recv_sem,
):
    devices = n_row * n_col
    edge_dev, width = cur_ref.shape
    half = width // 2
    tri = cen_ref.shape[1]
    cells = b_out.shape[1]
    slots = cells // devices
    n_cols = n_row * tri
    n_sweeps = w_ref.shape[0]
    side = 4
    my_row, my_col = lax.axis_index("row"), lax.axis_index("col")
    me = my_row * n_col + my_col
    mx, mc = lax.div(my_row, 2), lax.rem(my_row, 2)
    mz, my = lax.div(my_col, side), lax.rem(my_col, side)

    def flat_id(index):
        return (lax.div(index, n_col), lax.rem(index, n_col))

    def ahead(d):
        return flat_id(lax.rem(me + d, devices))

    def behind(d):
        return flat_id(lax.rem(me + devices - d, devices))

    def along_row(dx, dc):
        return (lax.rem(mx + dx, side) * 2 + lax.rem(mc + dc, 2), my_col)

    def along_col(dz, dy):
        return (my_row, lax.rem(mz + dz, side) * side + lax.rem(my + dy, side))

    sends, recvs = [0], [0]

    def new(count, many):
        count[0] += many
        return count[0] - many

    S_ROWC, S_COLC, S_LAB = (new(sends, 1) for _ in range(3))
    R_ROWC, R_COLC, R_LAB = (new(recvs, 1) for _ in range(3))
    S_A1, S_B1, S_A2, S_B2 = (new(sends, n_sweeps) for _ in range(4))
    S_B, S_Q, S_F = (new(sends, 2 * n_sweeps) for _ in range(3))
    R_B1, R_A2, R_B2 = (new(recvs, n_sweeps) for _ in range(3))
    R_B, R_Q2, R_F = (new(recvs, 2 * n_sweeps) for _ in range(3))
    R_A1 = new(recvs, n_sweeps * side)
    R_Q1 = new(recvs, 2 * n_sweeps * side)

    def remote(src, dst, s, r, device):
        return pltpu.make_async_remote_copy(
            src_ref=src, dst_ref=dst, send_sem=send_sem.at[s], recv_sem=recv_sem.at[r],
            device_id=device, device_id_type=MESH,
        )

    barrier = pltpu.get_barrier_semaphore()

    def greet(h, carry):
        for j in range(8):
            d = devices - 1 - h * 8 - j
            pl.semaphore_signal(barrier, inc=1, device_id=ahead(d), device_id_type=MESH)
        return carry

    lax.fori_loop(0, devices // 8 - 1, greet, 0)
    for d in range(1, 8):
        pl.semaphore_signal(barrier, inc=1, device_id=ahead(d), device_id_type=MESH)

    both = jnp.concatenate([inc_ref[0:1, :], inc_ref[1:2, :]], axis=1)
    n_con = both.shape[1]
    owner = lax.shift_right_logical(both, tri.bit_length() - 1)
    local = (both & (tri - 1)).astype(F32)
    rel = (owner - me + devices) & (devices - 1)
    hits = jnp.where(rel == iota((devices, n_con), 0), 1.0, 0.0)
    hits16 = hits.astype(BF16)
    earlier = jnp.where(iota((n_con, n_con), 0) < iota((n_con, n_con), 1), 1.0, 0.0).astype(BF16)
    before = jnp.dot(hits16, earlier, preferred_element_type=F32)
    rank = jnp.sum(hits * before, axis=0, keepdims=True)
    slot = rel.astype(F32) * float(slots) + rank
    marks = jnp.where(rank == iota((128, n_con), 0).astype(F32), local + 1.0, 0.0).astype(BF16)
    lab_flat[...] = lax.dot_general(
        hits16, marks, (((1,), (1,)), ((), ())), preferred_element_type=F32
    )
    slot_plus, slot_minus = slot[:, :edge_dev], slot[:, edge_dev:]

    def spread(d, carry):
        lab_out[d] = lab_flat[pl.ds(d, 1), :]
        return carry

    lax.fori_loop(0, devices, spread, 0)
    chunk = 256
    group = chunk // slots
    for c in range(2):
        cur[c] = cur_ref[:, c * half:(c + 1) * half]

    def part(h, size):
        return pl.ds(h * size if isinstance(h, int) else pl.multiple_of(h * size, size), size)

    def block(d):
        return part(d, slots)

    rest = pl.ds(slots, cells - slots)
    nobody = ahead(1)

    def fill_place(h, carry):
        at = (iota((chunk, edge_dev), 0) + h * chunk).astype(F32)
        rows = jnp.where(slot_plus == at, 1.0, 0.0) - jnp.where(slot_minus == at, 1.0, 0.0)
        place[part(h, chunk), :] = rows.astype(BF16)
        place_t[:, part(h, chunk)] = rows.T.astype(BF16)
        return carry

    lax.fori_loop(0, cells // chunk, fill_place, 0)

    def fill_out(c, h):
        at = part(h, chunk)
        b_out[c, at, :] = jnp.dot(place[at, :], cur[c], preferred_element_type=F32).astype(BF16)

    def first_of(h):
        return range(1 if isinstance(h, int) else 0, group)

    def send_out(sweep, c, h):
        for j in first_of(h):
            d = h * group + j
            remote(
                b_out.at[c, block(d)], b_in.at[sweep, c, block(d)],
                S_B + 2 * sweep + c, R_B + 2 * sweep + c, ahead(d),
            ).start()

    def all_chunks(one):
        one(0)

        def other(h, carry):
            one(h)
            return carry

        lax.fori_loop(1, cells // chunk, other, 0)

    def fill_first(h, carry):
        fill_out(0, h)
        fill_out(1, h)
        return carry

    lax.fori_loop(0, cells // chunk, fill_first, 0)
    pl.semaphore_wait(barrier, devices - 1)

    def send_row_cen(k, carry):
        to = along_col(lax.div(k, side) + 1, lax.rem(k, side) + 1)
        remote(cen_ref, row_cen.at[k], S_ROWC, R_ROWC, to).start()
        return carry

    def send_col_cen(r, carry):
        to = along_row(lax.rem(r, side), lax.div(r, side))
        remote(cen_ref, col_cen.at[r], S_COLC, R_COLC, to).start()
        return carry

    lax.fori_loop(1, n_row, send_col_cen, 0)
    lax.fori_loop(0, n_col - 1, send_row_cen, 0)

    def send_labels(h):
        for j in first_of(h):
            d = h * group + j
            remote(lab_out.at[d], lab_in.at[d], S_LAB, R_LAB, ahead(d)).start()

    def send_first(h):
        for j in first_of(h):
            d = h * group + j
            remote(b_out.at[:, block(d)], b_in.at[0, :, block(d)], S_B, R_B, ahead(d)).start()

    all_chunks(send_labels)
    all_chunks(send_first)
    b_in[0, :, 0:slots, :] = b_out[:, 0:slots, :]
    lab_in[0] = lab_out[0]
    row_cen[n_col - 1] = cen_ref[...]
    col_cen[0] = cen_ref[...]

    drop_rows = pl.ds(0, n_col - 1)
    drop_cols = pl.ds(1, n_row - 1)
    row_wait = remote(row_cen.at[drop_rows], row_cen.at[drop_rows], S_ROWC, R_ROWC, nobody)
    col_wait = remote(col_cen.at[drop_cols], col_cen.at[drop_cols], S_COLC, R_COLC, nobody)
    col_wait.wait_send()
    col_wait.wait_recv()
    for r in range(n_row):
        feat_col[:, r * tri:(r + 1) * tri] = features(col_cen[r], False)
    row_wait.wait_send()
    row_wait.wait_recv()
    for t in range(n_col):
        feat_row[:, t * tri:(t + 1) * tri] = features(row_cen[t], True)

    step = 128

    def make_tile(tile, k, base):
        for u in range(tri // step):
            at, here = part(k * (tri // step) + u, step), part((k - base) * (tri // step) + u, step)
            dist = lax.dot_general(
                feat_row[:, at], feat_col[...], (((0,), (0,)), ((), ())), preferred_element_type=F32
            )
            inv = lax.rsqrt(dist)
            turns = dist * inv
            r = turns - jnp.round(turns)
            s = r * r
            sine = r * horner(SIN, s, ROOT)
            cosine = horner(COS, s, -ROOT)
            tile[here, 0:n_cols] = (inv * (jnp.float32(AMP) - sine * sine)).astype(BF16)
            tile[here, n_cols:2 * n_cols] = (inv * (sine * cosine)).astype(BF16)

    def make_a(k, carry):
        make_tile(tile_a, k, 0)
        return carry

    n_a = n_col // 2
    cuts = (0, 4, 5, 6, 7, n_a)

    def more_tile(stage):
        lax.fori_loop(cuts[stage], cuts[stage + 1], make_a, 0)

    def fill_qq(sweep, c, r):
        at = pl.ds(r * tri, tri)
        below = pl.ds(n_cols + r * tri, tri)
        q = q_in[sweep, c, at, :]
        if c == 0:
            qq[at, :half] = q
            qq[below, half:] = q
        else:
            qq[at, half:] = q
            qq[below, :half] = -q

    def read_labels():
        labels = remote(
            lab_out.at[pl.ds(1, devices - 1)], lab_in.at[pl.ds(1, devices - 1)], S_LAB, R_LAB, nobody
        )
        labels.wait_send()
        labels.wait_recv()

        def gather(d, carry):
            lab_flat[pl.ds(d, 1), :] = lab_in[d]
            return carry

        lax.fori_loop(0, devices, gather, 0)
        widen = jnp.where(
            lax.div(iota((chunk, group), 0), slots) == iota((chunk, group), 1), 1.0, 0.0
        ).astype(BF16)
        keep = jnp.where(
            lax.rem(iota((chunk, 128), 0), slots) == iota((chunk, 128), 1), 1.0, 0.0
        )
        ones = jnp.ones((128, tri), BF16)
        target = (iota((chunk, tri), 1) + 1).astype(F32)

        def fill_pick(h, carry):
            here = lab_flat[part(h, group), :].astype(BF16)
            wide = jnp.dot(widen, here, preferred_element_type=F32) * keep
            label = jnp.dot(wide.astype(BF16), ones, preferred_element_type=F32)
            rows = jnp.where(label == target, 1.0, 0.0)
            pick[part(h, chunk), :] = rows.astype(BF16)
            pick_t[:, part(h, chunk)] = rows.T.astype(BF16)
            return carry

        lax.fori_loop(0, cells // chunk, fill_pick, 0)

    def charges_of(sweep):
        partner = along_row(0, 1)
        waits = []
        if sweep == 0:
            more_tile(0)
            read_labels()
        for c in range(2):
            at = 2 * sweep + c
            if sweep > 0:
                wait = remote(b_out.at[c, rest], b_in.at[sweep, c, rest], S_B + at, R_B + at, nobody)
                wait.wait_recv()
                waits.append(wait)
            elif c == 0:
                wait = remote(b_out.at[:, rest], b_in.at[0, :, rest], S_B, R_B, nobody)
                wait.wait_recv()
                waits.append(wait)
            q_in[sweep, c, 0:tri, :] = jnp.dot(
                pick_t[...], b_in[sweep, c], preferred_element_type=F32
            ).astype(BF16)
            mine = q_in.at[sweep, c, pl.ds(0, tri)]
            for dx in (2, 1, 3):
                remote(
                    mine, q_in.at[sweep, c, pl.ds(dx * tri, tri)],
                    S_Q + at, R_Q1 + at * side + dx, along_row(dx, 0),
                ).start()
            remote(mine, q_in.at[sweep, c, pl.ds(side * tri, tri)], S_Q + at, R_Q2 + at, partner).start()
            fill_qq(sweep, c, 0)
            if sweep == 0 and c == 1:
                more_tile(1)
                more_tile(2)
        for c in range(2):
            at = 2 * sweep + c
            for dx in (1, 3, 2):
                got = q_in.at[sweep, c, pl.ds(dx * tri, tri)]
                remote(got, got, S_Q + at, R_Q1 + at * side + dx, partner).wait_recv()
                remote(
                    got, q_in.at[sweep, c, pl.ds((side + dx) * tri, tri)], S_Q + at, R_Q2 + at, partner
                ).start()
                fill_qq(sweep, c, dx)
            if sweep == 0:
                more_tile(3 + c)
        for c in range(2):
            at = 2 * sweep + c
            far = q_in.at[sweep, c, pl.ds(side * tri, side * tri)]
            remote(far, far, S_Q + at, R_Q2 + at, nobody).wait_recv()
            for r in range(side, 2 * side):
                fill_qq(sweep, c, r)
            if c < len(waits):
                waits[c].wait_send()
            sent = q_in.at[sweep, c, pl.ds(tri, n_cols - tri)]
            remote(sent, sent, S_Q + at, R_Q2 + at, nobody).wait_send()

    def wait_for(ref, s, r):
        return remote(ref, ref, s, r, nobody)

    last = side - 1

    def finish_a(sweep, g):
        wait_for(p1a.at[sweep, g], S_A1 + sweep, R_A1 + sweep * side + g).wait_recv()
        total = own_a[g]
        for j in range(last):
            total = total + p1a[sweep, g, j].astype(F32)
        return total

    def finish_b(sweep, g):
        total = own_b[g]
        for j in range(last):
            total = total + p1b[sweep, j, g].astype(F32)
        return total

    def emit(sweep, k, value):
        k = jnp.int32(k)
        gz, gy = lax.div(k, side), lax.rem(k, side)
        left, right = value[:, :half], value[:, half:]

        @pl.when(gy < last)
        def _():
            rs_a[k] = left.astype(BF16)
            remote(
                rs_a.at[k], p1a.at[sweep, gz, gy], S_A1 + sweep, R_A1 + sweep * side + gz,
                along_col(0, last - gy),
            ).start()

        @pl.when(gz < last)
        def _():
            rs_b[k] = right.astype(BF16)
            remote(
                rs_b.at[k], p1b.at[sweep, gz, gy], S_B1 + sweep, R_B1 + sweep,
                along_col(last - gz, 0),
            ).start()

        @pl.when(gy == last)
        def _():
            own_a[gz] = left

        @pl.when(gz == last)
        def _():
            own_b[gy] = right

        @pl.when(jnp.logical_and(gy == last - 1, gz > 0))
        def _():
            g = gz - 1
            rs2a[g] = finish_a(sweep, g).astype(BF16)
            remote(
                rs2a.at[g], p2a.at[sweep, g], S_A2 + sweep, R_A2 + sweep, along_col(last - g, 0)
            ).start()

    for sweep in range(n_sweeps):
        charges_of(sweep)

        def close_b():
            wait_for(p1b.at[sweep], S_B1 + sweep, R_B1 + sweep).wait_recv()
            for g in range(last):
                rs2b[g] = finish_b(sweep, g).astype(BF16)
                remote(
                    rs2b.at[g], p2b.at[sweep, g], S_B2 + sweep, R_B2 + sweep, along_col(0, last - g)
                ).start()

        def upper(k, carry):
            value = jnp.dot(tile_a[part(k, tri), :], qq[...], preferred_element_type=F32)
            emit(sweep, k, value)
            return carry

        def lower(k, carry, more):
            value = jnp.dot(tile_b[part(k - n_a, tri), :], qq[...], preferred_element_type=F32)
            if more:
                make_tile(tile_b, k + 1, n_a)
            emit(sweep, k, value)
            return carry

        if sweep == 0:
            lax.fori_loop(0, n_a, upper, 0)
            make_tile(tile_b, n_a, n_a)
            lax.fori_loop(n_a, n_col - 1, functools.partial(lower, more=True), 0)
            close_b()
            lower(n_col - 1, 0, False)
        else:
            lax.fori_loop(0, n_a, upper, 0)
            lax.fori_loop(n_a, n_col, functools.partial(lower, more=False), 0)
            close_b()

        def answer(c):
            def one(h):
                at = part(h, chunk)
                f_out[c, at, :] = jnp.dot(pick[at, :], pot[c], preferred_element_type=F32).astype(BF16)
                for j in first_of(h):
                    d = h * group + j
                    remote(
                        f_out.at[c, block(d)], f_in.at[sweep, c, block(d)],
                        S_F + 2 * sweep + c, R_F + 2 * sweep + c, behind(d),
                    ).start()

            all_chunks(one)
            f_in[sweep, c, 0:slots, :] = f_out[c, 0:slots, :]
            if sweep == n_sweeps - 1:
                pot_ref[:, c * half:(c + 1) * half] = pot[c]

        left = finish_a(sweep, last)
        wait_for(p2a.at[sweep], S_A2 + sweep, R_A2 + sweep).wait_recv()
        for j in range(last):
            left = left + p2a[sweep, j].astype(F32)
        pot[0] = left.astype(BF16)
        answer(0)
        right = finish_b(sweep, last)
        wait_for(p2b.at[sweep], S_B2 + sweep, R_B2 + sweep).wait_recv()
        for j in range(last):
            right = right + p2b[sweep, j].astype(F32)
        pot[1] = right.astype(BF16)
        answer(1)
        wait_for(rs_a.at[pl.ds(0, last * side)], S_A1 + sweep, R_B1 + sweep).wait_send()
        wait_for(rs_b.at[pl.ds(0, last * side)], S_B1 + sweep, R_B1 + sweep).wait_send()
        wait_for(rs2a, S_A2 + sweep, R_A2 + sweep).wait_send()
        wait_for(rs2b, S_B2 + sweep, R_B2 + sweep).wait_send()
        for c in range(2):
            at = 2 * sweep + c
            f_wait = remote(f_out.at[c, rest], f_in.at[sweep, c, rest], S_F + at, R_F + at, nobody)
            f_wait.wait_recv()
            slope = jnp.dot(place_t[...], f_in[sweep, c], preferred_element_type=F32)
            updated = (cur[c].astype(F32) - w_ref[sweep] * slope).astype(BF16)
            if sweep == n_sweeps - 1:
                upd_ref[:, c * half:(c + 1) * half] = updated
            else:
                cur[c] = updated

                def next_out(h):
                    fill_out(c, h)
                    send_out(sweep + 1, c, h)

                all_chunks(next_out)
                b_in[sweep + 1, c, 0:slots, :] = b_out[c, 0:slots, :]
            f_wait.wait_send()


def solution(mesh):
    n_row, n_col = mesh.shape["row"], mesh.shape["col"]
    devices = n_row * n_col

    def per_device(currents, incidence, centroids, sweep_weights):
        edge_dev, width = currents.shape
        tri = centroids.shape[1]
        n_sweeps = sweep_weights.shape[0]
        slots = 16
        cells = devices * slots
        vm = pltpu.VMEM
        return pl.pallas_call(
            functools.partial(kernel, n_row, n_col),
            out_shape=(
                jax.ShapeDtypeStruct((edge_dev, width), BF16),
                jax.ShapeDtypeStruct((tri, width), BF16),
            ),
            in_specs=[pl.BlockSpec(memory_space=pltpu.VMEM)] * 3
            + [pl.BlockSpec(memory_space=pltpu.SMEM)],
            out_specs=(pl.BlockSpec(memory_space=pltpu.VMEM),) * 2,
            scratch_shapes=[
                vm((n_col * tri // 2, 2 * n_row * tri), BF16),
                vm((n_col * tri // 2, 2 * n_row * tri), BF16),
                vm((2, cells, width // 2), BF16),
                vm((n_sweeps, 2, cells, width // 2), BF16),
                vm((2, cells, width // 2), BF16),
                vm((n_sweeps, 2, cells, width // 2), BF16),
                vm((n_sweeps, 2, n_row * tri, width // 2), BF16),
                vm((2 * n_row * tri, width), BF16),
                vm((cells, edge_dev), BF16),
                vm((edge_dev, cells), BF16),
                vm((cells, tri), BF16),
                vm((tri, cells), BF16),
                vm((n_col, tri, width // 2), BF16),
                vm((n_col, tri, width // 2), BF16),
                vm((4, tri, width // 2), F32),
                vm((4, tri, width // 2), F32),
                vm((n_sweeps, 4, 3, tri, width // 2), BF16),
                vm((n_sweeps, 3, 4, tri, width // 2), BF16),
                vm((3, tri, width // 2), BF16),
                vm((3, tri, width // 2), BF16),
                vm((n_sweeps, 3, tri, width // 2), BF16),
                vm((n_sweeps, 3, tri, width // 2), BF16),
                vm((devices, 128), F32),
                vm((devices, 1, 128), F32),
                vm((devices, 1, 128), F32),
                vm((n_col, 3, tri), jnp.int32),
                vm((n_row, 3, tri), jnp.int32),
                vm((16, n_col * tri), BF16),
                vm((16, n_row * tri), BF16),
                vm((2, edge_dev, width // 2), BF16),
                vm((2, tri, width // 2), BF16),
                pltpu.SemaphoreType.DMA((3 + 10 * n_sweeps,)),
                pltpu.SemaphoreType.DMA((3 + 21 * n_sweeps,)),
            ],
            compiler_params=pltpu.CompilerParams(
                collective_id=0, has_side_effects=True, vmem_limit_bytes=66000000
            ),
            name="sweeps",
        )(currents, incidence, centroids, sweep_weights)

    in_specs = (P(("row", "col"), None), P(None, ("row", "col")), P(None, ("row", "col")), P())
    out_specs = (P(("row", "col"), None), P(("row", "col"), None))
    return jax.shard_map(
        per_device, mesh=mesh, in_specs=in_specs, out_specs=out_specs, check_vma=False
    )
```

time: 157 us -> 150 us (0.955)
  Pallas kernels: 154 us -> 147 us
    pallas_call x1, Pallas kernels: 154 us -> 147 us  [per_device(): pl.pallas_call(functools.partial(kernel, n_row, n_col), out_shape=(jax.Sh...]
where the time goes in v3:
time: 150 us
  Pallas kernels  147 us (98%)
  local copies, waits for them, and re-layouts  2.31 us (2%)
    pallas_call x1, Pallas kernels, per_device(): pl.pallas_call(functools.partial(kernel, n_row, n_col), out_shape=(jax.Sh...  147 us

profile of v3, /device:TPU:0, one launch (start us, length us, event | category | flops | bytes accessed | tf_op | source)
XLA Modules:
  0.0 149.6 jit_solution(12570561501135223771)
XLA Ops:
  0.6 146.6 %sweeps.1 = (bf16[384,256]{1,0:T(8,128)(2,1)}, bf16[256,256]{1,0:T(8,128)(2,1)}) custom-call(bf16[384,256]{1,0:T(8,128)(2,1)} %cur_ref.1, s32[2,384]{1,0:T(2,128)} %inc_ref.1, s32[3,256]{1,0:T(4,128)} %cen_ref.1, f32[2]{0:T(128)} %w_ref.1), custom_call_target="tpu_custom_call" | custom-call | tf_op jit(solution)/shard_map/sweeps/pallas_call | solution.py:520
  147.2 0.0 copy-start
  147.3 1.7 %copy.8 = bf16[384,256]{1,0:T(8,128)(2,1)} copy(bf16[384,256]{1,0:T(8,128)(2,1)} %get-tuple-element.4) | data formatting | bytes 393216
  148.9 0.0 copy-done
  148.9 0.7 copy.9
Async XLA Ops:
  147.2 1.7 %copy-start = (bf16[256,256]{1,0:T(8,128)(2,1)S(1)}, bf16[256,256]{1,0:T(8,128)(2,1)}, u32[]{:S(2)}) copy-start(bf16[256,256]{1,0:T(8,128)(2,1)} %get-tuple-element.5) | copy-start | bytes 393220

commit v4 on v3

--- a/solution.py
+++ b/solution.py
@@ -14,7 +14,7 @@
 AMP = 0.2 / 32.0
 ROOT = (2.0 * AMP) ** 0.5
 SIN = (3.14158202, -5.1671428, 2.54189902, -0.554636165)
-COS = (0.999999953, -4.93479286, 4.05841191, -1.33188016, 0.219696799)
+COS = (-0.11181640625, 0.55078125, -0.4453125, 0.1328125)
 
 
 def iota(shape, dim):
@@ -25,6 +25,13 @@
     acc = jnp.float32(coefs[-1] * scale)
     for c in coefs[-2::-1]:
         acc = acc * s + jnp.float32(c * scale)
+    return acc
+
+
+def horner16(coefs, s):
+    acc = BF16(coefs[-1])
+    for c in coefs[-2::-1]:
+        acc = acc * s + BF16(c)
     return acc
 
 
@@ -256,9 +263,9 @@
             r = turns - jnp.round(turns)
             s = r * r
             sine = r * horner(SIN, s, ROOT)
-            cosine = horner(COS, s, -ROOT)
+            cosine = horner16(COS, s.astype(BF16))
             tile[here, 0:n_cols] = (inv * (jnp.float32(AMP) - sine * sine)).astype(BF16)
-            tile[here, n_cols:2 * n_cols] = (inv * (sine * cosine)).astype(BF16)
+            tile[here, n_cols:2 * n_cols] = (inv * sine).astype(BF16) * cosine
 
     def make_a(k, carry):
         make_tile(tile_a, k, 0)

time: 150 us -> 147 us (0.980)
  Pallas kernels: 147 us -> 144 us
    pallas_call x1, Pallas kernels: 147 us -> 144 us  [per_device(): pl.pallas_call(functools.partial(kernel, n_row, n_col), out_shape=(jax.Sh...]
where the time goes in v4:
time: 147 us
  Pallas kernels  144 us (98%)
  local copies, waits for them, and re-layouts  2.31 us (2%)
    pallas_call x1, Pallas kernels, per_device(): pl.pallas_call(functools.partial(kernel, n_row, n_col), out_shape=(jax.Sh...  144 us

profile of v4, /device:TPU:0, one launch (start us, length us, event | category | flops | bytes accessed | tf_op | source)
XLA Modules:
  0.0 146.6 jit_solution(14383678162794713129)
XLA Ops:
  0.6 143.6 %sweeps.1 = (bf16[384,256]{1,0:T(8,128)(2,1)}, bf16[256,256]{1,0:T(8,128)(2,1)}) custom-call(bf16[384,256]{1,0:T(8,128)(2,1)} %cur_ref.1, s32[2,384]{1,0:T(2,128)} %inc_ref.1, s32[3,256]{1,0:T(4,128)} %cen_ref.1, f32[2]{0:T(128)} %w_ref.1), custom_call_target="tpu_custom_call" | custom-call | tf_op jit(solution)/shard_map/sweeps/pallas_call | solution.py:527
  144.3 0.0 copy-start
  144.3 1.7 %copy.8 = bf16[384,256]{1,0:T(8,128)(2,1)} copy(bf16[384,256]{1,0:T(8,128)(2,1)} %get-tuple-element.4) | data formatting | bytes 393216
  145.9 0.0 copy-done
  145.9 0.7 copy.9
Async XLA Ops:
  144.3 1.7 %copy-start = (bf16[256,256]{1,0:T(8,128)(2,1)S(1)}, bf16[256,256]{1,0:T(8,128)(2,1)}, u32[]{:S(2)}) copy-start(bf16[256,256]{1,0:T(8,128)(2,1)} %get-tuple-element.5) | copy-start | bytes 393220

commit v5 on v4

--- a/solution.py
+++ b/solution.py
@@ -271,8 +271,8 @@
         make_tile(tile_a, k, 0)
         return carry
 
-    n_a = n_col // 2
-    cuts = (0, 4, 5, 6, 7, n_a)
+    n_a = tile_a.shape[0] // tri
+    cuts = (0, 5, 6, 7, 8, n_a)
 
     def more_tile(stage):
         lax.fori_loop(cuts[stage], cuts[stage + 1], make_a, 0)
@@ -419,13 +419,20 @@
         def _():
             own_b[gy] = right
 
-        @pl.when(jnp.logical_and(gy == last - 1, gz > 0))
-        def _():
-            g = gz - 1
+        def close_a(g):
             rs2a[g] = finish_a(sweep, g).astype(BF16)
             remote(
                 rs2a.at[g], p2a.at[sweep, g], S_A2 + sweep, R_A2 + sweep, along_col(last - g, 0)
             ).start()
+
+        if sweep == 0:
+            @pl.when(jnp.logical_and(gy == last - 1, gz > 0))
+            def _():
+                close_a(gz - 1)
+        else:
+            @pl.when(jnp.logical_and(gz == last, gy < last))
+            def _():
+                close_a(gy)
 
     for sweep in range(n_sweeps):
         charges_of(sweep)
@@ -534,8 +541,8 @@
             + [pl.BlockSpec(memory_space=pltpu.SMEM)],
             out_specs=(pl.BlockSpec(memory_space=pltpu.VMEM),) * 2,
             scratch_shapes=[
-                vm((n_col * tri // 2, 2 * n_row * tri), BF16),
-                vm((n_col * tri // 2, 2 * n_row * tri), BF16),
+                vm((9 * tri, 2 * n_row * tri), BF16),
+                vm(((n_col - 9) * tri, 2 * n_row * tri), BF16),
                 vm((2, cells, width // 2), BF16),
                 vm((n_sweeps, 2, cells, width // 2), BF16),
                 vm((2, cells, width // 2), BF16),

time: 147 us -> 145 us (0.986)
  Pallas kernels: 144 us -> 142 us
    pallas_call x1, Pallas kernels: 144 us -> 142 us  [per_device(): pl.pallas_call(functools.partial(kernel, n_row, n_col), out_shape=(jax.Sh...]
where the time goes in v5:
time: 145 us
  Pallas kernels  142 us (98%)
  local copies, waits for them, and re-layouts  2.31 us (2%)
    pallas_call x1, Pallas kernels, per_device(): pl.pallas_call(functools.partial(kernel, n_row, n_col), out_shape=(jax.Sh...  142 us

profile of v5, /device:TPU:0, one launch (start us, length us, event | category | flops | bytes accessed | tf_op | source)
XLA Modules:
  0.0 144.5 jit_solution(7975682159992480261)
XLA Ops:
  0.6 141.6 %sweeps.1 = (bf16[384,256]{1,0:T(8,128)(2,1)}, bf16[256,256]{1,0:T(8,128)(2,1)}) custom-call(bf16[384,256]{1,0:T(8,128)(2,1)} %cur_ref.1, s32[2,384]{1,0:T(2,128)} %inc_ref.1, s32[3,256]{1,0:T(4,128)} %cen_ref.1, f32[2]{0:T(128)} %w_ref.1), custom_call_target="tpu_custom_call" | custom-call | tf_op jit(solution)/shard_map/sweeps/pallas_call | solution.py:534
  142.2 0.0 copy-start
  142.2 1.7 %copy.8 = bf16[384,256]{1,0:T(8,128)(2,1)} copy(bf16[384,256]{1,0:T(8,128)(2,1)} %get-tuple-element.4) | data formatting | bytes 393216
  143.9 0.0 copy-done
  143.9 0.7 copy.9
Async XLA Ops:
  142.2 1.7 %copy-start = (bf16[256,256]{1,0:T(8,128)(2,1)S(1)}, bf16[256,256]{1,0:T(8,128)(2,1)}, u32[]{:S(2)}) copy-start(bf16[256,256]{1,0:T(8,128)(2,1)} %get-tuple-element.5) | copy-start | bytes 393220
